TPU v7x, 128 devices: a whole 4x4x4 slice. The times are simulated.
128 devices in a mesh: front: 8 (over x, core), grp: 16 (over y, z).
Axes of the slice: x: 4, y: 4, z: 4, core: 2. Of those that a mesh axis runs over, the one named last changes fastest.
Arguments:
- contributions: bfloat16 [16384, 16384], P(('front', 'grp')), may hold values from -6 to 6
- sketch_matrix: bfloat16 [16384, 256], P(('front', 'grp')), may hold values from -0.046875 to 0.046875
- destinations: int32 [16384, 1], replicated, may hold values from 0 to 127; in each aligned block of 128 rows (0 to 127, 128 to 255, ...) at most 2 rows name the same one
- parent_rows: int32 [16384], replicated, may hold values from 0 to 1023
- front_sizes: int32 [8], P('front'), may hold values from 8192 to 16384
- leaf_skeleton: int32 [8, 16, 128], P('front', 'grp'), may hold values from 0 to 1023, as said below
- merge_skeleton: int32 [8, 14, 128], P('front'), may hold values from 0 to 255, as said below
Outputs:
- leaf_maps: float32 [8, 16384, 128], P('front', 'grp')
- node_maps: float32 [8, 16, 3, 256, 128], P('front', 'grp')
- top_rows: float32 [8, 16, 128, 256], P('front', 'grp')
Inputs may be any that keep to these rules, and one draw needn't show every extreme that they name: `destinations`: in the rows of one device no destination is named by more than 2 rows. `leaf_skeleton`: each row holds 128 different row numbers of a leaf block. `merge_skeleton`: each row holds 128 different positions of the stacked 2 * 128 rows.
All inputs are finite; a program needn't handle non-finite values.
Results may differ from a plain program's by a relative error of at most 0.003.
Values may be sent and summed in bfloat16 or wider, within the bound.
No kernel may reach another device: no remote copies, remote signals or barrier semaphores. Data moves between devices by JAX's collectives and lax.ppermute only.
A program may use at most 64 MiB of HBM per device.

v0:
```python
import jax
import jax.numpy as jnp
from jax import lax
from jax.sharding import PartitionSpec as P

PR_DEV = 1024
LEVELS = 3


def from_partner(block, axis, stride):
    count = lax.axis_size(axis)
    route = []
    for low in range(count):
        high = low | 1 << stride
        if high != low and high < count:
            route += [(low, high), (high, low)]
    return lax.ppermute(block, axis, route)


def ridge_map(rows, basis):
    gram = jnp.dot(basis, basis.T, precision=lax.Precision.HIGHEST)
    shift = 0.1 * jnp.mean(jnp.diagonal(gram)) + 1e-05
    ident = jnp.eye(gram.shape[0], dtype=jnp.float32)
    gram = gram + shift * ident
    approx = ident / jnp.trace(gram)
    for step in range(24):
        approx = jnp.dot(
            approx,
            2.0 * ident - jnp.dot(gram, approx, precision=lax.Precision.HIGHEST),
            precision=lax.Precision.HIGHEST,
        )
    right = jnp.dot(rows, basis.T, precision=lax.Precision.HIGHEST)
    return jnp.dot(right, approx, precision=lax.Precision.HIGHEST)


def select_rows(rows, index):
    picker = (index[:, None] == jnp.arange(rows.shape[0], dtype=jnp.int32)[None, :]).astype(
        jnp.float32
    )
    return jnp.dot(picker, rows, precision=lax.Precision.HIGHEST)


def local(
    contributions,
    sketch_matrix,
    destinations,
    parent_rows,
    front_sizes,
    leaf_skeleton,
    merge_skeleton,
):
    fronts = lax.axis_size("front")
    leaves = lax.axis_size("grp")
    devices = fronts * leaves
    grp_index = lax.axis_index("grp")
    myself = lax.axis_index("front") * leaves + grp_index
    rows_dev = contributions.shape[0]
    width = sketch_matrix.shape[1]
    capacity = 2 * rows_dev // devices
    sketch = jnp.dot(
        contributions,
        lax.all_gather(sketch_matrix, ("front", "grp"), axis=0, tiled=True),
        preferred_element_type=jnp.float32,
    )
    sketch = sketch.astype(jnp.bfloat16)
    every_dest = destinations[:, 0].reshape(devices, rows_dev)
    every_row = parent_rows.reshape(devices, rows_dev)
    mine = lax.dynamic_index_in_dim(every_dest, myself, 0, keepdims=False)
    owners = jnp.arange(devices, dtype=jnp.int32)
    hits = (mine[:, None] == owners[None, :]).astype(jnp.int32)
    before = jnp.cumsum(hits, axis=0) - hits
    slot_of = jnp.sum(before * hits, axis=1)
    keys = mine * capacity + slot_of
    placing = (keys[None, :] == jnp.arange(devices * capacity, dtype=jnp.int32)[:, None]).astype(
        jnp.bfloat16
    )
    packed = jnp.dot(placing, sketch, preferred_element_type=jnp.float32).astype(jnp.bfloat16)
    packed = packed.reshape(devices, capacity, width)
    arrived = lax.all_to_all(
        packed, ("front", "grp"), split_axis=0, concat_axis=0, tiled=True
    ).reshape(devices * capacity, width)
    landing = (every_dest == myself).astype(jnp.int32)
    slots = jnp.cumsum(landing, axis=1) - landing
    match = landing[:, None, :] * (
        slots[:, None, :] == jnp.arange(capacity, dtype=jnp.int32)[None, :, None]
    ).astype(jnp.int32)
    local_row = jnp.sum(match * every_row[:, None, :], axis=2)
    filled = jnp.sum(match, axis=2)
    where_to = jnp.where(filled > 0, local_row, -1).reshape(devices * capacity)
    adding = (jnp.arange(PR_DEV, dtype=jnp.int32)[:, None] == where_to[None, :]).astype(
        jnp.bfloat16
    )
    parent = jnp.dot(adding, arrived, preferred_element_type=jnp.float32)
    global_row = grp_index * PR_DEV + jnp.arange(PR_DEV, dtype=jnp.int32)
    parent = jnp.where((global_row < front_sizes[0])[:, None], parent, jnp.zeros_like(parent))
    basis = select_rows(parent, leaf_skeleton[0, 0])
    leaf_map = ridge_map(parent, basis)
    skeletons = merge_skeleton[0]
    level_maps = []
    current = basis
    for level in range(LEVELS):
        partner = from_partner(current, "grp", level)
        upper_side = grp_index >> level & 1 == 1
        first = jnp.where(upper_side, partner, current)
        second = jnp.where(upper_side, current, partner)
        stacked = jnp.concatenate([first, second], axis=0)
        node = leaves - (leaves >> level) + (grp_index >> level + 1)
        chosen = lax.dynamic_index_in_dim(skeletons, node, 0, keepdims=False)
        current = select_rows(stacked, chosen)
        level_maps.append(ridge_map(stacked, current))
    node_maps = jnp.stack(level_maps, axis=0)
    return (leaf_map[None], node_maps[None, None], current[None, None])


def solution(mesh):
    in_specs = (
        P(("front", "grp"), None),
        P(("front", "grp"), None),
        P(),
        P(),
        P("front"),
        P("front", "grp", None),
        P("front", None, None),
    )
    out_specs = (
        P("front", "grp", None),
        P("front", "grp", None, None, None),
        P("front", "grp", None, None),
    )
    return jax.shard_map(local, mesh=mesh, in_specs=in_specs, out_specs=out_specs, check_vma=False)
```

profile of v0, /device:TPU:1, one launch (start us, length us, event | category | flops | bytes accessed | tf_op | source)
XLA Modules:
  0.0 180.9 jit_solution(4281349015124919198)
XLA Ops:
  7.2 0.7 all-gather.2.cloned.1.call-update
  7.9 0.9 copy.16
  9.1 0.7 fusion.47
  11.1 1.0 select_reduce_fusion
  12.1 0.7 fusion.46
  12.8 71.7 %all-gather.2.cloned.1.call-done = bf16[16384,256]{1,0:T(8,128)(2,1)} async-done(((bf16[128,256]{1,0:T(8,128)(2,1)}), bf16[16384,256]{1,0:T(8,128)(2,1)}) %all-gather.2.cloned.1.call-update) | async-done | bytes 8388624 | tf_op jit(solution)/shard_map/all_gather | solution.py:62
  84.5 6.1 %convolution_convert_fusion = bf16[256,256]{1,0:T(8,128)(2,1)S(1)} fusion(bf16[128,16384]{1,0:T(8,128)(2,1)} %param.7, bf16[16384,256]{1,0:T(8,128)(2,1)} %all-gather.2.cloned.1.call-done, s32[128]{0:T(128)S(1)} %fusion.46), kind=kOutput, calls=%fused_computation.102 | convolution fusion | flops 1090650112 | bytes 12714496 | tf_op jit(solution)/shard_map/dot_general | solution.py:77
  90.6 0.7 reshape.69
  91.3 5.4 %all-to-all-start = ((bf16[128,2,256]{2,1,0:T(2,128)(2,1)}), bf16[128,2,256]{2,1,0:T(2,128)(2,1)S(1)}, u32[]{:S(2)}, u32[]{:S(2)}) async-start(bf16[128,2,256]{2,1,0:T(2,128)(2,1)} %reshape.69), calls=%async_computation | async-start | bytes 262144 | tf_op jit(solution)/shard_map/all_to_all | solution.py:79
  97.0 0.7 fusion.43
  97.7 9.0 %all-to-all-done = bf16[128,2,256]{2,1,0:T(2,128)(2,1)S(1)} async-done(((bf16[128,2,256]{2,1,0:T(2,128)(2,1)}), bf16[128,2,256]{2,1,0:T(2,128)(2,1)S(1)}, u32[]{:S(2)}, u32[]{:S(2)}) %all-to-all-start) | async-done | bytes 131104 | tf_op jit(solution)/shard_map/all_to_all | solution.py:79
  107.1 0.6 fusion.1
  107.7 0.8 collective-permute-start
  108.8 1.0 fusion.62
  109.8 1.2 gather_fusion
  111.0 0.6 reduce_sum.97
  112.3 0.6 select_reduce_fusion.4
  123.8 1.4 convolution_bitcast_fusion
  126.1 1.4 collective-permute-start.1
  127.5 1.2 gather_fusion.1
  128.7 0.6 reduce_sum.99
  130.0 0.6 select_reduce_fusion.3
  142.4 0.4 fusion.5
  142.7 0.7 collective-permute-start.2
  143.5 1.2 gather_fusion.2
  144.7 0.6 reduce_sum.101
  146.0 0.6 select_reduce_fusion.2
  158.3 0.4 fusion.3
  158.7 1.5 gather_fusion.3
  160.3 0.6 reduce_sum.103
  161.5 0.6 select_reduce_fusion.1
  173.3 0.8 maximum_bitcast_fusion
  (229 shorter events, 43.9 us)
Async XLA Ops:
  7.2 100.0 %copy-start.1 = (s32[1,1,128]{2,1,0:T(1,128)S(1)}, s32[1,1,128]{2,1,0:T(1,128)}, u32[]{:S(2)}) copy-start(s32[1,1,128]{2,1,0:T(1,128)} %param.12) | copy-start | bytes 1540
  7.2 77.3 %all-gather.2.cloned.1.call-start = ((), (), s32[]{:S(2)}) async-start(), calls=%async_computation.1 | async-start | bytes 8454144 | tf_op jit(solution)/shard_map/all_gather | solution.py:62
  91.3 15.4 %all-to-all-start = ((bf16[128,2,256]{2,1,0:T(2,128)(2,1)}), bf16[128,2,256]{2,1,0:T(2,128)(2,1)S(1)}, u32[]{:S(2)}, u32[]{:S(2)}) async-start(bf16[128,2,256]{2,1,0:T(2,128)(2,1)} %reshape.69), calls=%async_computation | async-start | bytes 262144 | tf_op jit(solution)/shard_map/all_to_all | solution.py:79
  107.7 17.5 %collective-permute-start = (f32[128,256]{1,0:T(8,128)S(1)}, f32[128,256]{1,0:T(8,128)S(1)}, u32[]{:S(2)}, u32[]{:S(2)}) collective-permute-start(f32[128,256]{1,0:T(8,128)S(1)} %fusion.1), channel_id=1, source_target_pairs={{0,1},{1,0},{2,3},{3,2},{4,5},{5,4},{6,7},{7,6},{8,9},{9,8},{10,11... | collective-permute-start | bytes 393224 | tf_op jit(solution)/shard_map/ppermute | solution.py:17
  126.1 15.7 %collective-permute-start.1 = (f32[128,256]{1,0:T(8,128)S(1)}, f32[128,256]{1,0:T(8,128)S(1)}, u32[]{:S(2)}, u32[]{:S(2)}) collective-permute-start(f32[128,256]{1,0:T(8,128)S(1)} %fusion.8), channel_id=1, source_target_pairs={{0,2},{2,0},{1,3},{3,1},{4,6},{6,4},{5,7},{7,5},{8,10},{10,8},{9,1... | collective-permute-start | bytes 393224 | tf_op jit(solution)/shard_map/ppermute | solution.py:17
  142.7 15.0 %collective-permute-start.2 = (f32[128,256]{1,0:T(8,128)S(1)}, f32[128,256]{1,0:T(8,128)S(1)}, u32[]{:S(2)}, u32[]{:S(2)}) collective-permute-start(f32[128,256]{1,0:T(8,128)S(1)} %fusion.6), channel_id=1, source_target_pairs={{0,4},{4,0},{1,5},{5,1},{2,6},{6,2},{3,7},{7,3},{8,12},{12,8},{9,1... | collective-permute-start | bytes 393224 | tf_op jit(solution)/shard_map/ppermute | solution.py:17
  158.1 16.0 %copy-start = (f32[128,256]{1,0:T(8,128)}, f32[128,256]{1,0:T(8,128)S(1)}, u32[]{:S(2)}) copy-start(f32[128,256]{1,0:T(8,128)S(1)} %fusion.4) | copy-start | bytes 393220
Sparse Core Ops, SparseCore 0:
  11.1 73.3 all-gather.1
where the time goes:
time: 181 us
  waiting for transfers between devices  81.5 us (45%)
  matrix products  52.4 us (29%)
  between operations  21.9 us (12%)
  local copies, waits for them, and re-layouts  8.81 us (5%)
  starting transfers between devices  8.28 us (5%)
  other arithmetic  8.05 us (4%)
    all_gather x1, waiting for transfers between devices, local(): lax.all_gather(sketch_matrix, ('front', 'grp'), axis=0, tiled=True)  71.7 us
    dot_general x96, matrix products, ridge_map(): jnp.dot(gram, approx, precision=lax.Precision.HIGHEST)  19.7 us
    dot_general x96, matrix products, ridge_map(): jnp.dot(approx, 2.0 * ident - jnp.dot(gram, approx, precision=lax.Precisi...  19.5 us
    all_to_all x1, waiting for transfers between devices, local(): lax.all_to_all(packed, ('front', 'grp'), split_axis=0, concat_axis=0, til...  9.02 us
    dot_general x1, matrix products, local(): jnp.dot(placing, sketch, preferred_element_type=jnp.float32)  6.12 us
    all_to_all x1, starting transfers between devices, local(): lax.all_to_all(packed, ('front', 'grp'), split_axis=0, concat_axis=0, til...  5.37 us
    gather x4, local copies, waits for them, and re-layouts, ridge_map(): shift = 0.1 * jnp.mean(jnp.diagonal(gram)) + 1e-05  5.28 us
  transfers between devices with their start and end apart: 5, of which 2 were waited for; matrix products, arithmetic and copies ran while one was open for 25% of the time, Pallas kernels for 0%

commit v1 on v0

v1 whole, which is shorter than its diff:
```python
import functools

import jax
import jax.numpy as jnp
from jax import lax
from jax.experimental import pallas as pl
from jax.experimental.pallas import tpu as pltpu
from jax.sharding import Mesh
from jax.sharding import PartitionSpec as P

PR_DEV = 1024
LEVELS = 3
ROWS = 128
WIDTH = 256
HALF = 128
K = 128
DOUBLINGS = 8
ALL = ("x", "core", "grp")
F32 = jnp.float32
BF16 = jnp.bfloat16
HIGH = lax.Precision.HIGHEST


def coords(device):
    front, grp = device // 16, device % 16
    return [front >> 1, grp >> 2, grp & 3], front & 1


def device_of(chip, core):
    return (chip[0] * 2 + core) * 16 + chip[1] * 4 + chip[2]


def route(axis, masks):
    pairs = []
    for device in range(128):
        chip, core = coords(device)
        chip[axis] ^= masks[core]
        pairs.append((device, device_of(chip, core)))
    return pairs


def core_route():
    pairs = []
    for device in range(128):
        chip, core = coords(device)
        pairs.append((device, device_of(chip, 1 - core)))
    return pairs


def send(value, pairs):
    return lax.ppermute(value, ALL, pairs)


def vmem():
    return pl.BlockSpec(memory_space=pltpu.VMEM)


def smem():
    return pl.BlockSpec(memory_space=pltpu.SMEM)


def hbm():
    return pl.BlockSpec(memory_space=pl.ANY)


def call(kernel, outs, args, specs, out_specs, scratch=(), name=None, flops=0, aliases=None, limit=6):
    return pl.pallas_call(
        kernel,
        out_shape=outs,
        in_specs=specs,
        out_specs=out_specs,
        scratch_shapes=list(scratch),
        input_output_aliases=aliases or {},
        cost_estimate=pl.CostEstimate(flops=flops, bytes_accessed=1 << 20, transcendentals=0),
        compiler_params=pltpu.CompilerParams(vmem_limit_bytes=limit << 20),
        name=name,
    )(*args)


def split3(value):
    hi = value.astype(BF16)
    rest = value - hi.astype(F32)
    mid = rest.astype(BF16)
    low = (rest - mid.astype(F32)).astype(BF16)
    return hi, mid, low


def pick(onehot, value):
    out = None
    for term in split3(value):
        part = jnp.dot(onehot, term, preferred_element_type=F32)
        out = part if out is None else out + part
    return out


def extract_kernel(where, full, out):
    out[...] = full[...]


def other_half(contributions, core):
    return pl.pallas_call(
        extract_kernel,
        out_shape=jax.ShapeDtypeStruct((ROWS, 8192), BF16),
        grid_spec=pltpu.PrefetchScalarGridSpec(
            num_scalar_prefetch=1,
            grid=(4,),
            in_specs=[pl.BlockSpec((ROWS, 2048), lambda i, s: (0, 2 * i + 1 - s[0]))],
            out_specs=pl.BlockSpec((ROWS, 2048), lambda i, s: (0, i)),
        ),
        compiler_params=pltpu.CompilerParams(vmem_limit_bytes=4 << 20),
        name="other_half",
    )(core.reshape(1), contributions)


def piece_offset(where, order, piece):
    core = where[3]
    first, second = jnp.where(core == 0, 1, 3), jnp.where(core == 0, 3, 1)
    chip = [where[0], where[1], where[2]]
    for step, axis in enumerate(order):
        if (piece >> (2 * step)) & 1:
            chip[axis] = chip[axis] ^ first
        if (piece >> (2 * step + 1)) & 1:
            chip[axis] = chip[axis] ^ second
    inside = chip[1] * 4 + chip[2]
    whole = ((chip[0] * 2 + core) * 16 + inside) * 128
    half = (chip[0] * 16 + inside) * 128
    return pl.multiple_of(whole, 128), pl.multiple_of(half, 128)


ORDERS = ((0, 1, 2), (1, 2, 0))


def partial_products(where, own, received, pieces, first):
    columns = []
    for order, piece in zip(ORDERS, pieces):
        total = [None, None]
        for j in range(0, 32, 2):
            spot = [piece_offset(where, order, first + j), piece_offset(where, order, first + j + 1)]
            right = piece[j : j + 2].reshape(256, HALF)
            for side, source in enumerate((own, received)):
                left = jnp.concatenate([source[:, pl.ds(s[side], 128)] for s in spot], axis=1)
                part = jnp.dot(left, right, preferred_element_type=F32)
                total[side] = part if total[side] is None else total[side] + part
        columns.append(jnp.concatenate(total, axis=0))
    return jnp.concatenate(columns, axis=1)


def first_kernel(where, full, received, a, b, out):
    out[...] = partial_products(where, full, received, (a, b), 0)


def second_kernel(where, keys, full, received, a, b, acc, keep, give):
    total = acc[...] + partial_products(where, full, received, (a, b), 32)
    core = where[3]
    spots = lax.broadcasted_iota(jnp.int32, (256, 256), 0)
    key = keys[...]
    here = (key == spots + core * 256).astype(F32).astype(BF16)
    there = (key == spots + (1 - core) * 256).astype(F32).astype(BF16)
    keep[...] = pick(here, total)
    give[...] = pick(there, total)


def finish_kernel(keep, given, out):
    rows = (keep[...] + given[...]).astype(BF16).reshape(16, 16, WIDTH)
    for copy in range(4):
        out[:, copy] = rows


def join_kernel(a, b, out):
    count = a.shape[0]
    out[:count] = a[...]
    out[count:] = b[...]


def matches(column, row):
    return (column == row).astype(F32).astype(BF16)


def basis_kernel(arrived, landing, keys, out):
    out[...] = jnp.dot(
        matches(keys[...], landing[...]), arrived[...], preferred_element_type=F32
    )


def split2(value):
    hi = value.astype(BF16)
    return hi, (value - hi.astype(F32)).astype(BF16)


def mul(a, b):
    (ah, al), (bh, bl) = split2(a), split2(b)
    wide = jnp.dot(
        jnp.concatenate([ah, al], axis=1),
        jnp.concatenate([bh, bh], axis=0),
        preferred_element_type=F32,
    )
    return wide + jnp.dot(ah, bl, preferred_element_type=F32)


def mul_t(a, b, precision=None):
    dims = (((1,), (1,)), ((), ()))
    if precision is not None:
        return lax.dot_general(a, b, dims, precision=precision, preferred_element_type=F32)
    (ah, al), (bh, bl) = split2(a), split2(b)
    out = None
    for p, q in ((ah, bh), (ah, bl), (al, bh)):
        part = lax.dot_general(p, q, dims, preferred_element_type=F32)
        out = part if out is None else out + part
    return out


def inverses(bases):
    row = lax.broadcasted_iota(jnp.int32, (K, K), 0)
    col = lax.broadcasted_iota(jnp.int32, (K, K), 1)
    ident = (row == col).astype(F32)
    grams = [mul_t(s, s, HIGH) for s in bases]
    state = []
    for index, gram in enumerate(grams):
        trace = jnp.sum(jnp.sum(gram * ident, axis=0, keepdims=True), axis=1, keepdims=True)
        widest = jnp.max(jnp.sum(jnp.abs(gram), axis=0, keepdims=True), axis=1, keepdims=True)
        low = trace * (0.1 / K) + 1e-5
        gram = gram + low * ident
        grams[index] = gram
        high = jnp.maximum(low + jnp.minimum(trace, widest), 2.0 * low)
        scale = 2.0 / (low + high)
        ratio = (high - low) / (high + low)
        residual = ident - scale * gram
        state.append((scale, ratio, residual))
    for index, (scale, ratio, residual) in enumerate(state):
        square = ratio * ratio
        ratio = square / (2.0 - square)
        approx = ((1.0 + ratio) * scale) * (ident + residual)
        residual = (1.0 + ratio) * mul(residual, residual) - ratio * ident
        state[index] = (approx, ratio, residual)
    for step in range(1, DOUBLINGS):
        for index, (approx, ratio, residual) in enumerate(state):
            square = ratio * ratio
            ratio = square / (2.0 - square)
            if step + 1 < DOUBLINGS:
                both = mul(jnp.concatenate([approx, residual], axis=0), residual)
                approx = (1.0 + ratio) * (approx + both[:K])
                residual = (1.0 + ratio) * both[K:] - ratio * ident
            else:
                approx = (1.0 + ratio) * (approx + mul(approx, residual))
            state[index] = (approx, ratio, residual)
    results = []
    for gram, (approx, ratio, residual) in zip(grams, state):
        fix = ident - jnp.dot(gram, approx, precision=HIGH, preferred_element_type=F32)
        results.append((approx, fix))
    return results


def times_inverse(right, approx, fix):
    first = mul(right, approx)
    return first + mul(first, fix)


def choose(flag, first, second):
    return jnp.where(flag == 1, second, first)


def lower_kernel(flags, arrived, landing, own_landing, keys, top, leaf_out, out, built, sem):
    rows = arrived[...]
    stacks = jnp.dot(matches(keys[...], landing[...]), rows, preferred_element_type=F32)
    first, second = stacks[: 2 * K], stacks[2 * K :]
    leaf = choose(flags[0], first[:K], first[K:])
    node = choose(flags[1], second[:K], second[K:])
    bases = [leaf, node, top[...]]
    row = lax.broadcasted_iota(jnp.int32, (256, 1024), 0)
    col = lax.broadcasted_iota(jnp.int32, (256, 1024), 1)
    spot = (row >> 2) * 16 + flags[3] * 4 + (row & 3)
    mine = jnp.dot(matches(spot, col), rows, preferred_element_type=F32)
    rights = [mul_t(v, s) for v, s in zip((mine, first, second), bases)]
    maps = [times_inverse(r, *pair) for r, pair in zip(rights, inverses(bases))]
    for level in range(2):
        built[level] = maps[level + 1]
    copy = pltpu.make_async_copy(built, out.at[:2], sem)
    copy.start()
    spots = lax.broadcasted_iota(jnp.int32, (PR_DEV, 256), 0)
    leaf_out[0] = pick(matches(spots, own_landing[...]), maps[0])
    copy.wait()


def upper_kernel(flags, chosen, current, partner, previous, out, top, built, sem):
    mine, other = current[...], partner[...]
    stacked = jnp.concatenate(
        [choose(flags[2], mine, other), choose(flags[2], other, mine)], axis=0
    )
    spots = lax.broadcasted_iota(jnp.int32, (K, 2 * K), 1)
    basis = pick(matches(chosen[...], spots), stacked)
    top[...] = basis
    right = mul_t(stacked, basis)
    built[...] = times_inverse(right, *inverses([basis])[0])
    copy = pltpu.make_async_copy(built, out.at[2], sem)
    copy.start()
    copy.wait()


def join(a, b, limit):
    return call(
        join_kernel,
        jax.ShapeDtypeStruct((2 * a.shape[0],) + a.shape[1:], a.dtype),
        (a, b),
        [vmem(), vmem()],
        vmem(),
        name="join",
        limit=limit,
    )


def local(contributions, sketch_matrix, destinations, parent_rows, front_sizes, leaf_skeleton, merge_skeleton):
    x, core, grp = lax.axis_index("x"), lax.axis_index("core"), lax.axis_index("grp")
    y, z = grp >> 2, grp & 3
    myself = (x * 2 + core) * 16 + grp
    where = jnp.stack([x, y, z, core]).astype(jnp.int32)

    held = [sketch_matrix[None, :, :HALF], sketch_matrix[None, :, HALF:]]
    side = core
    for step in range(3):
        for half in range(2):
            masks = (1, 3) if half == 0 else (3, 1)
            arriving = [send(held[c], route(ORDERS[c][step], masks)) for c in range(2)]
            if step == 2 and half == 1:
                extra = arriving
            else:
                held = [join(h, r, 4) for h, r in zip(held, arriving)]
            if step == 1 and half == 1:
                (
                    held,
                    side,
                    destinations,
                    parent_rows,
                    front_sizes,
                    leaf_skeleton,
                    merge_skeleton,
                ) = lax.optimization_barrier(
                    (
                        held,
                        core,
                        destinations,
                        parent_rows,
                        front_sizes,
                        leaf_skeleton,
                        merge_skeleton,
                    )
                )
    received = send(other_half(contributions, side), core_route())

    every_dest = destinations[:, 0].reshape(128, ROWS)
    every_row = parent_rows.reshape(128, ROWS)
    later = jnp.arange(ROWS)[:, None] < jnp.arange(ROWS)[None, :]

    def keys_of(device, source_core):
        dest = lax.dynamic_index_in_dim(every_dest, device, 0, keepdims=False)
        same = (dest[:, None] == dest[None, :]) & later
        rank = jnp.sum(same.astype(jnp.int32), axis=0)
        chip = (dest >> 5) * 16 + (dest & 15)
        return ((dest >> 4) & 1) * 256 + chip * 4 + source_core * 2 + rank

    keys = jnp.concatenate(
        [keys_of(myself, core), keys_of((x * 2 + 1 - core) * 16 + grp, 1 - core)]
    ).reshape(1, 256)
    leaves = jnp.arange(4, dtype=jnp.int32)[:, None, None]
    mine = every_dest[None] == leaves + (myself - z)
    before = jnp.dot(
        mine.reshape(512, ROWS).astype(BF16), later.astype(BF16), preferred_element_type=F32
    ).reshape(4, 128, ROWS)
    spots = [
        jnp.sum(jnp.where(mine & (before == slot), every_row[None] + 1, 0), axis=2) - 1
        for slot in range(2)
    ]
    landing = jnp.stack(spots, axis=2)
    live = front_sizes[0] - (y * 4 + leaves) * PR_DEV
    landing = jnp.where((landing >= 0) & (landing < live), landing + leaves * PR_DEV, -1)
    landing = landing.reshape(4, 4, 2, 16, 2).transpose(1, 3, 0, 2, 4)
    own_landing = lax.dynamic_index_in_dim(landing, z, 2, keepdims=False).reshape(1, 256)
    own_landing = jnp.where(own_landing >= 0, own_landing - z * PR_DEV, -1)
    landing = landing.reshape(1, 1024)

    flags = jnp.stack([z & 1, (z >> 1) & 1, y & 1, z]).astype(jnp.int32)
    near = leaf_skeleton.reshape(K) + z * PR_DEV
    side_keys = send(near, route(2, (1, 1)))
    pair = jnp.where(z & 1 == 1, jnp.stack([side_keys, near]), jnp.stack([near, side_keys]))
    pair = pair.reshape(2 * K)
    far = send(pair, route(2, (3, 3)))
    far = far.reshape(2 * K)

    def chosen_of(node):
        return lax.dynamic_index_in_dim(merge_skeleton[0], node, 0, keepdims=False)

    def taken(values, index):
        hit = index[:, None] == jnp.arange(2 * K, dtype=jnp.int32)[None, :]
        return jnp.sum(jnp.where(hit, values[None, :], 0), axis=1)

    low = taken(pair, chosen_of(grp >> 1))
    high = taken(far, chosen_of((grp >> 1) ^ 1))
    swap = (z >> 1) & 1 == 1
    middle = jnp.where(swap, jnp.stack([high, low]), jnp.stack([low, high])).reshape(2 * K)
    top_keys = taken(middle, chosen_of(8 + (grp >> 2))).reshape(K, 1)
    stack_keys = jnp.concatenate([pair, middle]).reshape(4 * K, 1)
    chosen = chosen_of(12 + (grp >> 3)).reshape(K, 1)

    held, keys, landing, own_landing, stack_keys, top_keys, chosen, flags = lax.optimization_barrier(
        (held, keys, landing, own_landing, stack_keys, top_keys, chosen, flags)
    )
    square = jax.ShapeDtypeStruct((256, 256), F32)
    acc = call(
        first_kernel,
        square,
        (where, contributions, received, held[0], held[1]),
        [smem()] + [vmem()] * 4,
        vmem(),
        name="sketch_first",
        flops=1 << 29,
        limit=12,
    )
    keep, give = call(
        second_kernel,
        (square, square),
        (where, keys, contributions, received, extra[0], extra[1], acc),
        [smem()] + [vmem()] * 6,
        (vmem(), vmem()),
        name="sketch_second",
        flops=1 << 29,
        limit=12,
    )
    packed = call(
        finish_kernel,
        jax.ShapeDtypeStruct((16, 4, 16, WIDTH), BF16),
        (keep, send(give, core_route())),
        [vmem(), vmem()],
        vmem(),
        name="finish",
    )
    arrived = lax.all_to_all(
        packed.reshape(64, 16, WIDTH), ("x", "grp"), split_axis=0, concat_axis=0, tiled=True
    ).reshape(1024, WIDTH)

    rows = jax.ShapeDtypeStruct((K, WIDTH), F32)
    current = call(
        basis_kernel, rows, (arrived, landing, top_keys), [vmem()] * 3, vmem(), name="basis", flops=1 << 24
    )
    partner = send(current, route(1, (1, 1)))
    shape = jax.ShapeDtypeStruct((LEVELS, 2 * K, K), F32)
    leaf_map, maps = call(
        lower_kernel,
        (jax.ShapeDtypeStruct((1, PR_DEV, K), F32), shape),
        (flags, arrived, landing, own_landing, stack_keys, current),
        [smem()] + [vmem()] * 5,
        (vmem(), hbm()),
        [pltpu.VMEM((2, 2 * K, K), F32), pltpu.SemaphoreType.DMA],
        name="lower_maps",
        flops=1 << 31,
        limit=12,
    )
    maps, top = call(
        upper_kernel,
        (shape, rows),
        (flags, chosen, current, partner, maps),
        [smem(), vmem(), vmem(), vmem(), hbm()],
        (hbm(), vmem()),
        [pltpu.VMEM((2 * K, K), F32), pltpu.SemaphoreType.DMA],
        name="upper_map",
        flops=1 << 31,
        aliases={4: 0},
    )
    return (leaf_map, maps[None, None], top[None, None])


def solution(mesh):
    inner = Mesh(mesh.devices.reshape(4, 2, 16), ("x", "core", "grp"))
    in_specs = (
        P(ALL, None),
        P(ALL, None),
        P(),
        P(),
        P(("x", "core")),
        P(("x", "core"), "grp", None),
        P(("x", "core"), None, None),
    )
    out_specs = (
        P(("x", "core"), "grp", None),
        P(("x", "core"), "grp", None, None, None),
        P(("x", "core"), "grp", None, None),
    )
    return jax.shard_map(local, mesh=inner, in_specs=in_specs, out_specs=out_specs, check_vma=False)
```

time: 181 us -> 105 us (0.58)
  waiting for transfers between devices: 81.5 us -> 28.4 us
  matrix products: 52.4 us -> 0.31 us
  starting transfers between devices: 8.28 us -> 40.9 us
  Pallas kernels: 0 us -> 23 us
  between operations: 21.9 us -> 1.78 us
  other arithmetic: 8.05 us -> 1.32 us
    all_gather x1 -> x0, waiting for transfers between devices: 71.7 us -> none  [local(): lax.all_gather(sketch_matrix, ('front', 'grp'), axis=0, tiled=True)]
    dot_general x210 -> x1, matrix products: 52.4 us -> 0.31 us  [local(): jnp.dot(mine.reshape(512, ROWS).astype(BF16), later.astype(BF16), preferr...]
    ppermute x3 -> x17, starting transfers between devices: 2.88 us -> 35.2 us  [send(): return lax.ppermute(value, ALL, pairs)]
    pallas_call x0 -> x17, Pallas kernels: none -> 23 us  [the longest x16 21 us: call(): pl.pallas_call(kernel, out_shape=outs, in_specs=specs, out_specs=out_spec...]
    ppermute x3 -> x17, waiting for transfers between devices: 0.01 us -> 16.8 us  [send(): return lax.ppermute(value, ALL, pairs)]
    unnamed x4 -> x15, local copies, waits for them, and re-layouts: 0.01 us -> 5.43 us
    gather x4 -> x0, local copies, waits for them, and re-layouts: 5.28 us -> none  [ridge_map(): shift = 0.1 * jnp.mean(jnp.diagonal(gram)) + 1e-05]
    reduce_sum x10 -> x5, other arithmetic: 6.04 us -> 0.87 us  [the longest x3 0.51 us: taken(): return jnp.sum(jnp.where(hit, values[None, :], 0), axis=1)]
  transfers between devices with their start and end apart: 5 -> 18, of which waited for: 2 -> 11; matrix products, arithmetic and copies ran while one was open for 25% -> 4% of each run, Pallas kernels for 0% -> 13%
where the time goes in v1:
time: 105 us; the launch traced here: 104 us
  starting transfers between devices  40.9 us (39%)
  waiting for transfers between devices  28.4 us (27%)
  Pallas kernels  23 us (22%)
  local copies, waits for them, and re-layouts  8.61 us (8%)
  between operations  1.78 us (2%)
  other arithmetic  1.32 us (1%)
    ppermute x17, starting transfers between devices, send(): return lax.ppermute(value, ALL, pairs)  35.2 us
    pallas_call x16, Pallas kernels, call(): pl.pallas_call(kernel, out_shape=outs, in_specs=specs, out_specs=out_spec...  21 us
    ppermute x17, waiting for transfers between devices, send(): return lax.ppermute(value, ALL, pairs)  16.8 us
    all_to_all x1, waiting for transfers between devices, local(): lax.all_to_all(packed.reshape(64, 16, WIDTH), ('x', 'grp'), split_axis=0,...  11.6 us
    all_to_all x1, starting transfers between devices, local(): lax.all_to_all(packed.reshape(64, 16, WIDTH), ('x', 'grp'), split_axis=0,...  5.76 us
    unnamed x15, local copies, waits for them, and re-layouts  5.43 us
  transfers between devices with their start and end apart: 18, of which 11 were waited for; matrix products, arithmetic and copies ran while one was open for 4% of the time, Pallas kernels for 13%

profile of v1, /device:TPU:1, one launch (start us, length us, event | category | flops | bytes accessed | tf_op | source)
XLA Modules:
  0.0 104.3 jit_solution(16434388842195493970)
XLA Ops:
  1.5 3.6 %collective-permute-start.4 = (bf16[1,128,128]{2,1,0:T(8,128)(2,1)S(1)}, bf16[1,128,128]{2,1,0:T(8,128)(2,1)S(1)}, u32[]{:S(2)}, u32[]{:S(2)}) collective-permute-start(bf16[1,128,128]{2,1,0:T(8,128)(2,1)S(1)} %get-tuple-element.55.a), channel_id=1, source_target_pairs={{0,4},{1,5},{2,6},{3,7},{4,0},{5,1},{6,2},{7,3},{8,12},{9,13},{10,... | collective-permute-start | bytes 98312 | tf_op jit(solution)/shard_map/ppermute | solution.py:51
  5.0 2.5 %collective-permute-start = (bf16[1,128,128]{2,1,0:T(8,128)(2,1)S(1)}, bf16[1,128,128]{2,1,0:T(8,128)(2,1)S(1)}, u32[]{:S(2)}, u32[]{:S(2)}) collective-permute-start(bf16[1,128,128]{2,1,0:T(8,128)(2,1)S(1)} %get-tuple-element.56.a), channel_id=1, source_target_pairs={{0,32},{1,33},{2,34},{3,35},{4,36},{5,37},{6,38},{7,39},{8,40},{9,... | collective-permute-start | bytes 98312 | tf_op jit(solution)/shard_map/ppermute | solution.py:51
  7.6 1.4 %collective-permute-done.b = bf16[1,128,128]{2,1,0:T(8,128)(2,1)S(1)} collective-permute-done((bf16[1,128,128]{2,1,0:T(8,128)(2,1)S(1)}, bf16[1,128,128]{2,1,0:T(8,128)(2,1)S(1)}, u32[]{:S(2)}, u32[]{:S(2)}) %collective-permute-start) | collective-permute-done | bytes 32800 | tf_op jit(solution)/shard_map/ppermute | solution.py:51
  9.3 1.4 %collective-permute-done.5.b = bf16[2,128,128]{2,1,0:T(8,128)(2,1)S(1)} collective-permute-done((bf16[2,128,128]{2,1,0:T(8,128)(2,1)S(1)}, bf16[2,128,128]{2,1,0:T(8,128)(2,1)S(1)}, u32[]{:S(2)}, u32[]{:S(2)}) %collective-permute-start.5) | collective-permute-done | bytes 65568 | tf_op jit(solution)/shard_map/ppermute | solution.py:51
  10.7 3.8 %collective-permute-start.6 = (bf16[4,128,128]{2,1,0:T(8,128)(2,1)S(1)}, bf16[4,128,128]{2,1,0:T(8,128)(2,1)S(1)}, u32[]{:S(2)}, u32[]{:S(2)}) collective-permute-start(bf16[4,128,128]{2,1,0:T(8,128)(2,1)S(1)} %join.15.a), channel_id=1, source_target_pairs={{0,1},{1,0},{2,3},{3,2},{4,5},{5,4},{6,7},{7,6},{8,9},{9,8},{10,11... | collective-permute-start | bytes 393224 | tf_op jit(solution)/shard_map/ppermute | solution.py:51
  14.6 1.5 %collective-permute-start.2 = (bf16[4,128,128]{2,1,0:T(8,128)(2,1)S(1)}, bf16[4,128,128]{2,1,0:T(8,128)(2,1)S(1)}, u32[]{:S(2)}, u32[]{:S(2)}) collective-permute-start(bf16[4,128,128]{2,1,0:T(8,128)(2,1)S(1)} %join.11.a), channel_id=1, source_target_pairs={{0,4},{1,5},{2,6},{3,7},{4,0},{5,1},{6,2},{7,3},{8,12},{9,13},{10,... | collective-permute-start | bytes 393224 | tf_op jit(solution)/shard_map/ppermute | solution.py:51
  16.1 0.8 collective-permute-done.6.b
  17.0 2.7 %collective-permute-done.2.b = bf16[4,128,128]{2,1,0:T(8,128)(2,1)S(1)} collective-permute-done((bf16[4,128,128]{2,1,0:T(8,128)(2,1)S(1)}, bf16[4,128,128]{2,1,0:T(8,128)(2,1)S(1)}, u32[]{:S(2)}, u32[]{:S(2)}) %collective-permute-start.2) | collective-permute-done | bytes 131104 | tf_op jit(solution)/shard_map/ppermute | solution.py:51
  20.6 1.6 %collective-permute-done.7.b = bf16[8,128,128]{2,1,0:T(8,128)(2,1)S(1)} collective-permute-done((bf16[8,128,128]{2,1,0:T(8,128)(2,1)S(1)}, bf16[8,128,128]{2,1,0:T(8,128)(2,1)S(1)}, u32[]{:S(2)}, u32[]{:S(2)}) %collective-permute-start.7) | collective-permute-done | bytes 262176 | tf_op jit(solution)/shard_map/ppermute | solution.py:51
  22.3 3.0 %collective-permute-done.3.b = bf16[8,128,128]{2,1,0:T(8,128)(2,1)S(1)} collective-permute-done((bf16[8,128,128]{2,1,0:T(8,128)(2,1)S(1)}, bf16[8,128,128]{2,1,0:T(8,128)(2,1)S(1)}, u32[]{:S(2)}, u32[]{:S(2)}) %collective-permute-start.3) | collective-permute-done | bytes 262176 | tf_op jit(solution)/shard_map/ppermute | solution.py:51
  25.3 0.8 join.13.a
  27.1 1.8 %collective-permute-start.9 = (bf16[16,128,128]{2,1,0:T(8,128)(2,1)S(1)}, bf16[16,128,128]{2,1,0:T(8,128)(2,1)S(1)}, u32[]{:S(2)}, u32[]{:S(2)}) collective-permute-start(bf16[16,128,128]{2,1,0:T(8,128)(2,1)S(1)} %join.17.a), channel_id=1, source_target_pairs={{0,32},{1,33},{2,34},{3,35},{4,36},{5,37},{6,38},{7,39},{8,40},{9,... | collective-permute-start | bytes 1572872 | tf_op jit(solution)/shard_map/ppermute | solution.py:51
  28.9 2.2 %collective-permute-start.8 = (bf16[16,128,128]{2,1,0:T(8,128)(2,1)}, bf16[16,128,128]{2,1,0:T(8,128)(2,1)S(1)}, u32[]{:S(2)}, u32[]{:S(2)}) collective-permute-start(bf16[16,128,128]{2,1,0:T(8,128)(2,1)} %join.13.a), channel_id=1, source_target_pairs={{0,1},{1,0},{2,3},{3,2},{4,5},{5,4},{6,7},{7,6},{8,9},{9,8},{10,11... | collective-permute-start | bytes 1572872 | tf_op jit(solution)/shard_map/ppermute | solution.py:51
  31.1 2.2 %copy-done = bf16[128,16384]{1,0:T(8,128)(2,1)S(1)} copy-done((bf16[128,16384]{1,0:T(8,128)(2,1)S(1)}, bf16[128,16384]{1,0:T(8,128)(2,1)}, u32[]{:S(2)}) %copy-start) | copy-done | bytes 4194328
  33.3 2.0 %other_half.1 = bf16[128,8192]{1,0:T(8,128)(2,1)} custom-call(s32[1]{0:T(128)} %bitcast.31.where, bf16[128,16384]{1,0:T(8,128)(2,1)S(1)} %copy-done), custom_call_target="tpu_custom_call" | custom-call | tf_op jit(solution)/shard_map/other_half/pallas_call | solution.py:101
  35.3 3.5 %collective-permute-start.12 = (bf16[128,8192]{1,0:T(8,128)(2,1)}, bf16[128,8192]{1,0:T(8,128)(2,1)S(1)}, u32[]{:S(2)}, u32[]{:S(2)}) collective-permute-start(bf16[128,8192]{1,0:T(8,128)(2,1)} %other_half.1), channel_id=1, source_target_pairs={{0,16},{1,17},{2,18},{3,19},{4,20},{5,21},{6,22},{7,23},{8,24},{9,... | collective-permute-start | bytes 6291464 | tf_op jit(solution)/shard_map/ppermute | solution.py:51
  39.2 1.0 copy-done.3
  41.0 2.1 %join.18.a = bf16[32,128,128]{2,1,0:T(8,128)(2,1)} custom-call(bf16[16,128,128]{2,1,0:T(8,128)(2,1)} %join.13.a, bf16[16,128,128]{2,1,0:T(8,128)(2,1)S(1)} %collective-permute-done.8.b), custom_call_target="tpu_custom_call" | custom-call | bytes 1048576 | tf_op jit(solution)/shard_map/join/pallas_call | solution.py:67
  45.0 2.4 %collective-permute-start.11 = (s32[256]{0:T(256)S(1)}, s32[256]{0:T(256)S(1)}, u32[]{:S(2)}, u32[]{:S(2)}) collective-permute-start(s32[256]{0:T(256)S(1)} %fusion.11), channel_id=1, source_target_pairs={{0,3},{1,2},{2,1},{3,0},{4,7},{5,6},{6,5},{7,4},{8,11},{9,10},{10,... | collective-permute-start | bytes 3080 | tf_op jit(solution)/shard_map/ppermute | solution.py:51
  47.6 1.6 %collective-permute-done.11 = s32[256]{0:T(256)S(1)} collective-permute-done((s32[256]{0:T(256)S(1)}, s32[256]{0:T(256)S(1)}, u32[]{:S(2)}, u32[]{:S(2)}) %collective-permute-start.11) | collective-permute-done | bytes 1056 | tf_op jit(solution)/shard_map/ppermute | solution.py:51
  49.6 2.2 %copy-done.1 = bf16[128,16384]{1,0:T(8,128)(2,1)S(1)} copy-done((bf16[128,16384]{1,0:T(8,128)(2,1)S(1)}, bf16[128,16384]{1,0:T(8,128)(2,1)}, u32[]{:S(2)}) %copy-start.1) | copy-done | bytes 4194328
  51.7 2.5 %sketch_first.1.acc = f32[256,256]{1,0:T(8,128)S(1)} custom-call(s32[4]{0:T(128)S(1)} %pad_add_fusion.3.where, bf16[128,16384]{1,0:T(8,128)(2,1)S(1)} %copy-done.1, bf16[128,8192]{1,0:T(8,128)(2,1)S(1)} %collective-permute-done.12.received, bf16[32,128,128]{2,1,0:T(8,128)(2,1)} %join.18.a, bf16[32,128,128]{2,1,0:T(8,128)(2,1)S(1)} %join.19.b), custom_call_target="tpu_custom_call" | custom-call | flops 536870912 | bytes 1048576 | tf_op jit(solution)/shard_map/sketch_first/pallas_call | solution.py:67
  54.4 2.9 %collective-permute-done.13.a = bf16[32,128,128]{2,1,0:T(8,128)(2,1)} collective-permute-done((bf16[32,128,128]{2,1,0:T(8,128)(2,1)}, bf16[32,128,128]{2,1,0:T(8,128)(2,1)}, u32[]{:S(2)}, u32[]{:S(2)}) %collective-permute-start.13) | collective-permute-done | bytes 1048608 | tf_op jit(solution)/shard_map/ppermute | solution.py:51
  57.3 3.3 %sketch_second.1 = (f32[256,256]{1,0:T(8,128)S(1)}, f32[256,256]{1,0:T(8,128)S(1)}) custom-call(s32[4]{0:T(128)S(1)} %pad_add_fusion.3.where, s32[1,256]{1,0:T(1,128)S(1)} %bitcast.60, bf16[128,16384]{1,0:T(8,128)(2,1)S(1)} %copy-done.1, bf16[128,8192]{1,0:T(8,128)(2,1)S(1)} %collective-permute-done.12.received, ...), custom_call_target="tpu_custom_call" | custom-call | flops 536870912 | bytes 1048576 | tf_op jit(solution)/shard_map/sketch_second/pallas_call | solution.py:67
  60.6 11.5 %collective-permute-start.15 = (f32[256,256]{1,0:T(8,128)S(1)}, f32[256,256]{1,0:T(8,128)S(1)}, u32[]{:S(2)}, u32[]{:S(2)}) collective-permute-start(f32[256,256]{1,0:T(8,128)S(1)} %get-tuple-element.39), channel_id=1, source_target_pairs={{0,16},{1,17},{2,18},{3,19},{4,20},{5,21},{6,22},{7,23},{8,24},{9,... | collective-permute-start | bytes 786440 | tf_op jit(solution)/shard_map/ppermute | solution.py:51
  72.1 1.2 %collective-permute-done.15.given = f32[256,256]{1,0:T(8,128)S(1)} collective-permute-done((f32[256,256]{1,0:T(8,128)S(1)}, f32[256,256]{1,0:T(8,128)S(1)}, u32[]{:S(2)}, u32[]{:S(2)}) %collective-permute-start.15) | collective-permute-done | bytes 262176 | tf_op jit(solution)/shard_map/ppermute | solution.py:51
  73.3 0.8 finish.1
  74.1 5.8 %all-to-all-start = ((bf16[64,16,256]{2,1,0:T(8,128)(2,1)}), bf16[64,16,256]{2,1,0:T(8,128)(2,1)S(1)}, u32[]{:S(2)}, u32[]{:S(2)}) async-start(bf16[64,16,256]{2,1,0:T(8,128)(2,1)} %bitcast.32), calls=%async_computation | async-start | bytes 1048576 | tf_op jit(solution)/shard_map/all_to_all | solution.py:435
  80.3 11.6 %all-to-all-done = bf16[64,16,256]{2,1,0:T(8,128)(2,1)S(1)} async-done(((bf16[64,16,256]{2,1,0:T(8,128)(2,1)}), bf16[64,16,256]{2,1,0:T(8,128)(2,1)S(1)}, u32[]{:S(2)}, u32[]{:S(2)}) %all-to-all-start) | async-done | bytes 524320 | tf_op jit(solution)/shard_map/all_to_all | solution.py:435
  92.1 1.0 collective-permute-start.16
  93.1 6.3 %lower_maps.1 = (f32[1,1024,128]{2,1,0:T(8,128)}, f32[3,256,128]{2,1,0:T(8,128)}) custom-call(s32[4]{0:T(128)S(1)} %pad_add_fusion.2.flags, bf16[1024,256]{1,0:T(8,128)(2,1)S(1)} %bitcast.59, s32[1,1024]{1,0:T(1,128)S(1)} %reshape.196.landing, s32[1,256]{1,0:T(1,128)S(1)} %select_n.102.own_landing, s32[512,1]{1,0:T(8,128)S(1)} %copy.30.keys, ...), custom_call_target="tpu_custom_call" | custom-call | flops 2147483648 | bytes 1048576 | tf_op jit(solution)/shard_map/lower_maps/pallas_call | solution.py:67
  99.4 4.7 %upper_map.1 = (f32[3,256,128]{2,1,0:T(8,128)}, f32[128,256]{1,0:T(8,128)}) custom-call(s32[4]{0:T(128)S(1)} %pad_add_fusion.2.flags, s32[128,1]{1,0:T(8,128)S(1)} %copy.31.chosen, f32[128,256]{1,0:T(8,128)S(1)} %basis.1.top.current, f32[128,256]{1,0:T(8,128)S(1)} %collective-permute-done.16.partner, ...), custom_call_target="tpu_custom_call", output_to_operand_aliasing={{0}: (4, {})} | custom-call | flops 2147483648 | bytes 1048576 | tf_op jit(solution)/shard_map/upper_map/pallas_call | solution.py:67
  (73 shorter events, 6.9 us)
Async XLA Ops:
  0.6 25.5 %copy-start.6 = (s32[1,1,128]{2,1,0:T(1,128)S(1)}, s32[1,1,128]{2,1,0:T(1,128)}, u32[]{:S(2)}) copy-start(s32[1,1,128]{2,1,0:T(1,128)} %param.12) | copy-start | bytes 1540
  0.6 25.5 %copy-start.4 = (s32[16384,1]{0,1:T(1,128)S(1)}, s32[16384,1]{0,1:T(1,128)}, u32[]{:S(2)}) copy-start(s32[16384,1]{0,1:T(1,128)} %param.9) | copy-start | bytes 196612
  1.5 6.0 %collective-permute-start.4 = (bf16[1,128,128]{2,1,0:T(8,128)(2,1)S(1)}, bf16[1,128,128]{2,1,0:T(8,128)(2,1)S(1)}, u32[]{:S(2)}, u32[]{:S(2)}) collective-permute-start(bf16[1,128,128]{2,1,0:T(8,128)(2,1)S(1)} %get-tuple-element.55.a), channel_id=1, source_target_pairs={{0,4},{1,5},{2,6},{3,7},{4,0},{5,1},{6,2},{7,3},{8,12},{9,13},{10,... | collective-permute-start | bytes 98312 | tf_op jit(solution)/shard_map/ppermute | solution.py:51
  5.0 21.2 %copy-start.5 = (s32[16384]{0:T(1024)S(1)}, s32[16384]{0:T(1024)}, u32[]{:S(2)}) copy-start(s32[16384]{0:T(1024)} %param.10) | copy-start | bytes 196612
  5.0 4.0 %collective-permute-start = (bf16[1,128,128]{2,1,0:T(8,128)(2,1)S(1)}, bf16[1,128,128]{2,1,0:T(8,128)(2,1)S(1)}, u32[]{:S(2)}, u32[]{:S(2)}) collective-permute-start(bf16[1,128,128]{2,1,0:T(8,128)(2,1)S(1)} %get-tuple-element.56.a), channel_id=1, source_target_pairs={{0,32},{1,33},{2,34},{3,35},{4,36},{5,37},{6,38},{7,39},{8,40},{9,... | collective-permute-start | bytes 98312 | tf_op jit(solution)/shard_map/ppermute | solution.py:51
  7.5 3.2 %collective-permute-start.5 = (bf16[2,128,128]{2,1,0:T(8,128)(2,1)S(1)}, bf16[2,128,128]{2,1,0:T(8,128)(2,1)S(1)}, u32[]{:S(2)}, u32[]{:S(2)}) collective-permute-start(bf16[2,128,128]{2,1,0:T(8,128)(2,1)S(1)} %join.14.a), channel_id=1, source_target_pairs={{0,12},{1,13},{2,14},{3,15},{4,8},{5,9},{6,10},{7,11},{8,4},{9,5},... | collective-permute-start | bytes 196616 | tf_op jit(solution)/shard_map/ppermute | solution.py:51
  9.0 5.6 %collective-permute-start.1 = (bf16[2,128,128]{2,1,0:T(8,128)(2,1)S(1)}, bf16[2,128,128]{2,1,0:T(8,128)(2,1)S(1)}, u32[]{:S(2)}, u32[]{:S(2)}) collective-permute-start(bf16[2,128,128]{2,1,0:T(8,128)(2,1)S(1)} %join.10.a), channel_id=1, source_target_pairs={{0,96},{1,97},{2,98},{3,99},{4,100},{5,101},{6,102},{7,103},{8,104... | collective-permute-start | bytes 196616 | tf_op jit(solution)/shard_map/ppermute | solution.py:51
  10.7 6.2 %collective-permute-start.6 = (bf16[4,128,128]{2,1,0:T(8,128)(2,1)S(1)}, bf16[4,128,128]{2,1,0:T(8,128)(2,1)S(1)}, u32[]{:S(2)}, u32[]{:S(2)}) collective-permute-start(bf16[4,128,128]{2,1,0:T(8,128)(2,1)S(1)} %join.15.a), channel_id=1, source_target_pairs={{0,1},{1,0},{2,3},{3,2},{4,5},{5,4},{6,7},{7,6},{8,9},{9,8},{10,11... | collective-permute-start | bytes 393224 | tf_op jit(solution)/shard_map/ppermute | solution.py:51
  14.6 5.1 %collective-permute-start.2 = (bf16[4,128,128]{2,1,0:T(8,128)(2,1)S(1)}, bf16[4,128,128]{2,1,0:T(8,128)(2,1)S(1)}, u32[]{:S(2)}, u32[]{:S(2)}) collective-permute-start(bf16[4,128,128]{2,1,0:T(8,128)(2,1)S(1)} %join.11.a), channel_id=1, source_target_pairs={{0,4},{1,5},{2,6},{3,7},{4,0},{5,1},{6,2},{7,3},{8,12},{9,13},{10,... | collective-permute-start | bytes 393224 | tf_op jit(solution)/shard_map/ppermute | solution.py:51
  16.9 5.3 %collective-permute-start.7 = (bf16[8,128,128]{2,1,0:T(8,128)(2,1)S(1)}, bf16[8,128,128]{2,1,0:T(8,128)(2,1)S(1)}, u32[]{:S(2)}, u32[]{:S(2)}) collective-permute-start(bf16[8,128,128]{2,1,0:T(8,128)(2,1)S(1)} %join.16.a), channel_id=1, source_target_pairs={{0,3},{1,2},{2,1},{3,0},{4,7},{5,6},{6,5},{7,4},{8,11},{9,10},{10,... | collective-permute-start | bytes 786440 | tf_op jit(solution)/shard_map/ppermute | solution.py:51
  19.7 5.6 %collective-permute-start.3 = (bf16[8,128,128]{2,1,0:T(8,128)(2,1)S(1)}, bf16[8,128,128]{2,1,0:T(8,128)(2,1)S(1)}, u32[]{:S(2)}, u32[]{:S(2)}) collective-permute-start(bf16[8,128,128]{2,1,0:T(8,128)(2,1)S(1)} %join.12.a), channel_id=1, source_target_pairs={{0,12},{1,13},{2,14},{3,15},{4,8},{5,9},{6,10},{7,11},{8,4},{9,5},... | collective-permute-start | bytes 786440 | tf_op jit(solution)/shard_map/ppermute | solution.py:51
  22.3 13.0 %copy-start.2 = (bf16[16,128,128]{2,1,0:T(8,128)(2,1)}, bf16[16,128,128]{2,1,0:T(8,128)(2,1)S(1)}, u32[]{:S(2)}) copy-start(bf16[16,128,128]{2,1,0:T(8,128)(2,1)S(1)} %join.17.a) | copy-start | bytes 1572868
  26.1 18.9 %collective-permute-start.10 = (s32[128]{0:T(128)S(1)}, s32[128]{0:T(128)S(1)}, u32[]{:S(2)}, u32[]{:S(2)}) collective-permute-start(s32[128]{0:T(128)S(1)} %get-tuple-element.61), channel_id=1, source_target_pairs={{0,1},{1,0},{2,3},{3,2},{4,5},{5,4},{6,7},{7,6},{8,9},{9,8},{10,11... | collective-permute-start | bytes 1544 | tf_op jit(solution)/shard_map/ppermute | solution.py:51
  27.1 12.1 %collective-permute-start.9 = (bf16[16,128,128]{2,1,0:T(8,128)(2,1)S(1)}, bf16[16,128,128]{2,1,0:T(8,128)(2,1)S(1)}, u32[]{:S(2)}, u32[]{:S(2)}) collective-permute-start(bf16[16,128,128]{2,1,0:T(8,128)(2,1)S(1)} %join.17.a), channel_id=1, source_target_pairs={{0,32},{1,33},{2,34},{3,35},{4,36},{5,37},{6,38},{7,39},{8,40},{9,... | collective-permute-start | bytes 1572872 | tf_op jit(solution)/shard_map/ppermute | solution.py:51
  28.9 12.1 %collective-permute-start.8 = (bf16[16,128,128]{2,1,0:T(8,128)(2,1)}, bf16[16,128,128]{2,1,0:T(8,128)(2,1)S(1)}, u32[]{:S(2)}, u32[]{:S(2)}) collective-permute-start(bf16[16,128,128]{2,1,0:T(8,128)(2,1)} %join.13.a), channel_id=1, source_target_pairs={{0,1},{1,0},{2,3},{3,2},{4,5},{5,4},{6,7},{7,6},{8,9},{9,8},{10,11... | collective-permute-start | bytes 1572872 | tf_op jit(solution)/shard_map/ppermute | solution.py:51
  31.1 2.2 %copy-start = (bf16[128,16384]{1,0:T(8,128)(2,1)S(1)}, bf16[128,16384]{1,0:T(8,128)(2,1)}, u32[]{:S(2)}) copy-start(bf16[128,16384]{1,0:T(8,128)(2,1)} %full.5) | copy-start | bytes 12582916
  35.3 14.2 %collective-permute-start.12 = (bf16[128,8192]{1,0:T(8,128)(2,1)}, bf16[128,8192]{1,0:T(8,128)(2,1)S(1)}, u32[]{:S(2)}, u32[]{:S(2)}) collective-permute-start(bf16[128,8192]{1,0:T(8,128)(2,1)} %other_half.1), channel_id=1, source_target_pairs={{0,16},{1,17},{2,18},{3,19},{4,20},{5,21},{6,22},{7,23},{8,24},{9,... | collective-permute-start | bytes 6291464 | tf_op jit(solution)/shard_map/ppermute | solution.py:51
  39.2 1.0 copy-start.3
  40.3 14.1 %collective-permute-start.14 = (bf16[32,128,128]{2,1,0:T(8,128)(2,1)S(1)}, bf16[32,128,128]{2,1,0:T(8,128)(2,1)}, u32[]{:S(2)}, u32[]{:S(2)}) collective-permute-start(bf16[32,128,128]{2,1,0:T(8,128)(2,1)S(1)} %join.19.b), channel_id=1, source_target_pairs={{0,96},{1,97},{2,98},{3,99},{4,100},{5,101},{6,102},{7,103},{8,104... | collective-permute-start | bytes 3145736 | tf_op jit(solution)/shard_map/ppermute | solution.py:51
  43.1 14.3 %collective-permute-start.13 = (bf16[32,128,128]{2,1,0:T(8,128)(2,1)}, bf16[32,128,128]{2,1,0:T(8,128)(2,1)}, u32[]{:S(2)}, u32[]{:S(2)}) collective-permute-start(bf16[32,128,128]{2,1,0:T(8,128)(2,1)} %join.18.a), channel_id=1, source_target_pairs={{0,3},{1,2},{2,1},{3,0},{4,7},{5,6},{6,5},{7,4},{8,11},{9,10},{10,... | collective-permute-start | bytes 3145736 | tf_op jit(solution)/shard_map/ppermute | solution.py:51
  45.0 4.1 %collective-permute-start.11 = (s32[256]{0:T(256)S(1)}, s32[256]{0:T(256)S(1)}, u32[]{:S(2)}, u32[]{:S(2)}) collective-permute-start(s32[256]{0:T(256)S(1)} %fusion.11), channel_id=1, source_target_pairs={{0,3},{1,2},{2,1},{3,0},{4,7},{5,6},{6,5},{7,4},{8,11},{9,10},{10,... | collective-permute-start | bytes 3080 | tf_op jit(solution)/shard_map/ppermute | solution.py:51
  49.5 2.2 %copy-start.1 = (bf16[128,16384]{1,0:T(8,128)(2,1)S(1)}, bf16[128,16384]{1,0:T(8,128)(2,1)}, u32[]{:S(2)}) copy-start(bf16[128,16384]{1,0:T(8,128)(2,1)} %full.5) | copy-start | bytes 12582916
  60.6 12.6 %collective-permute-start.15 = (f32[256,256]{1,0:T(8,128)S(1)}, f32[256,256]{1,0:T(8,128)S(1)}, u32[]{:S(2)}, u32[]{:S(2)}) collective-permute-start(f32[256,256]{1,0:T(8,128)S(1)} %get-tuple-element.39), channel_id=1, source_target_pairs={{0,16},{1,17},{2,18},{3,19},{4,20},{5,21},{6,22},{7,23},{8,24},{9,... | collective-permute-start | bytes 786440 | tf_op jit(solution)/shard_map/ppermute | solution.py:51
  74.1 17.7 %all-to-all-start = ((bf16[64,16,256]{2,1,0:T(8,128)(2,1)}), bf16[64,16,256]{2,1,0:T(8,128)(2,1)S(1)}, u32[]{:S(2)}, u32[]{:S(2)}) async-start(bf16[64,16,256]{2,1,0:T(8,128)(2,1)} %bitcast.32), calls=%async_computation | async-start | bytes 1048576 | tf_op jit(solution)/shard_map/all_to_all | solution.py:435
  92.1 7.3 %collective-permute-start.16 = (f32[128,256]{1,0:T(8,128)S(1)}, f32[128,256]{1,0:T(8,128)S(1)}, u32[]{:S(2)}, u32[]{:S(2)}) collective-permute-start(f32[128,256]{1,0:T(8,128)S(1)} %basis.1.top.current), channel_id=1, source_target_pairs={{0,4},{1,5},{2,6},{3,7},{4,0},{5,1},{6,2},{7,3},{8,12},{9,13},{10,... | collective-permute-start | bytes 393224 | tf_op jit(solution)/shard_map/ppermute | solution.py:51

commit v2 on v1

v2 whole, which is shorter than its diff:
```python
import jax
import jax.numpy as jnp
from jax import lax
from jax.experimental import pallas as pl
from jax.experimental.pallas import tpu as pltpu
from jax.sharding import Mesh
from jax.sharding import PartitionSpec as P


PR_DEV = 1024
LEVELS = 3
ROWS = 128
WIDTH = 256
HALF = 128
K = 128
DOUBLINGS = 8
ALL = ("x", "core", "grp")
F32 = jnp.float32
BF16 = jnp.bfloat16
HIGH = lax.Precision.HIGHEST


def coords(device):
    front, grp = device // 16, device % 16
    return [front >> 1, grp >> 2, grp & 3], front & 1


def device_of(chip, core):
    return (chip[0] * 2 + core) * 16 + chip[1] * 4 + chip[2]


def route(axis, masks):
    pairs = []
    for device in range(128):
        chip, core = coords(device)
        chip[axis] ^= masks[core]
        pairs.append((device, device_of(chip, core)))
    return pairs


def core_route():
    pairs = []
    for device in range(128):
        chip, core = coords(device)
        pairs.append((device, device_of(chip, 1 - core)))
    return pairs


def send(value, pairs):
    return lax.ppermute(value, ALL, pairs)


def vmem():
    return pl.BlockSpec(memory_space=pltpu.VMEM)


def smem():
    return pl.BlockSpec(memory_space=pltpu.SMEM)


def hbm():
    return pl.BlockSpec(memory_space=pl.ANY)


def call(kernel, outs, args, specs, out_specs, scratch=(), flops=0, aliases=None, limit=6):
    return pl.pallas_call(
        kernel,
        out_shape=outs,
        in_specs=specs,
        out_specs=out_specs,
        scratch_shapes=list(scratch),
        input_output_aliases=aliases or {},
        cost_estimate=pl.CostEstimate(flops=flops, bytes_accessed=1 << 20, transcendentals=0),
        compiler_params=pltpu.CompilerParams(vmem_limit_bytes=limit << 20),
    )(*args)


def split3(value):
    hi = value.astype(BF16)
    rest = value - hi.astype(F32)
    mid = rest.astype(BF16)
    low = (rest - mid.astype(F32)).astype(BF16)
    return hi, mid, low


def pick(onehot, value):
    out = None
    for term in split3(value):
        part = jnp.dot(onehot, term, preferred_element_type=F32)
        out = part if out is None else out + part
    return out


def extract_kernel(where, full, give, held, sems):
    core = where[3]
    loads, stores = [], []
    for x in range(4):
        spot = pl.multiple_of((x * 2 + 1 - core) * 2048, 2048)
        inside = held.at[:, pl.ds(x * 2048, 2048)]
        loads.append(pltpu.make_async_copy(full.at[:, pl.ds(spot, 2048)], inside, sems.at[x]))
        stores.append(
            pltpu.make_async_copy(inside, give.at[:, pl.ds(x * 2048, 2048)], sems.at[4 + x])
        )
    for load in loads:
        load.start()
    for load, store in zip(loads, stores):
        load.wait()
        store.start()
    for store in stores:
        store.wait()


def piece_offset(where, order, piece):
    core = where[3]
    first, second = jnp.where(core == 0, 1, 3), jnp.where(core == 0, 3, 1)
    chip = [where[0], where[1], where[2]]
    for step, axis in enumerate(order):
        if (piece >> (2 * step)) & 1:
            chip[axis] = chip[axis] ^ first
        if (piece >> (2 * step + 1)) & 1:
            chip[axis] = chip[axis] ^ second
    inside = chip[1] * 4 + chip[2]
    return pl.multiple_of((chip[0] * 16 + inside) * 128, 128)


ORDERS = ((2, 0, 1), (2, 1, 0))


def products(where, source, chains, first):
    columns = []
    for order, pieces in zip(ORDERS, chains):
        total = None
        for block, piece in enumerate(pieces):
            for j in range(0, 16, 2):
                number = first + 16 * block + j
                spots = [piece_offset(where, order, number + k) for k in range(2)]
                right = piece[j : j + 2].reshape(256, HALF)
                left = jnp.concatenate([source[:, pl.ds(s, 128)] for s in spots], axis=1)
                part = jnp.dot(left, right, preferred_element_type=F32)
                total = part if total is None else total + part
        columns.append(total)
    return jnp.concatenate(columns, axis=1)


def partial_products(where, own, received, chains, first):
    halves = [products(where, source, chains, first) for source in (own, received)]
    return jnp.concatenate(halves, axis=0)


def first_kernel(where, full, received, a, b, out, own, sems):
    core = where[3]
    loads = []
    for x in range(4):
        spot = pl.multiple_of((x * 2 + core) * 2048, 2048)
        loads.append(
            pltpu.make_async_copy(
                full.at[:, pl.ds(spot, 2048)], own.at[:, pl.ds(x * 2048, 2048)], sems.at[x]
            )
        )
    for load in loads:
        load.start()
    out[ROWS:] = products(where, received, ((a,), (b,)), 0)
    for load in loads:
        load.wait()
    out[:ROWS] = products(where, own, ((a,), (b,)), 0)


def middle_kernel(where, own, received, a, c, b, d, acc, out):
    out[...] = acc[...] + partial_products(where, own, received, ((a, c), (b, d)), 16)


def second_kernel(where, keys, own, received, a, b, acc, keep, give):
    total = acc[...] + partial_products(where, own, received, ((a,), (b,)), 48)
    core = where[3]
    spots = lax.broadcasted_iota(jnp.int32, (256, 256), 0)
    key = keys[...]
    here = (key == spots + core * 256).astype(F32).astype(BF16)
    there = (key == spots + (1 - core) * 256).astype(F32).astype(BF16)
    keep[...] = pick(here, total)
    give[...] = pick(there, total)


def finish_kernel(keep, given, out):
    rows = (keep[...] + given[...]).astype(BF16).reshape(16, 16, WIDTH)
    for copy in range(4):
        out[:, copy] = rows


def join_kernel(a, b, out):
    count = a.shape[0]
    out[:count] = a[...]
    out[count:] = b[...]


def index_kernel(
    place, dest, rows, line_keys, merge, keys, landing, own_landing, stack_keys, top_keys, chosen
):
    myself, core, z, live, grp = (place[i] for i in range(5))
    sub = lax.broadcasted_iota(jnp.int32, (ROWS, ROWS), 0)
    lane = lax.broadcasted_iota(jnp.int32, (ROWS, ROWS), 1)
    for side in range(2):
        device = myself if side == 0 else myself + 16 - 32 * core
        row = dest[pl.ds(device, 1), :]
        wide = jnp.broadcast_to(row, (ROWS, ROWS))
        tall = wide.astype(F32).T.astype(jnp.int32)
        earlier = jnp.where((tall == wide) & (sub < lane), 1, 0)
        rank = jnp.sum(earlier, axis=0, keepdims=True)
        source = core if side == 0 else 1 - core
        chip = (row >> 5) * 16 + (row & 15)
        keys[:, side * ROWS : (side + 1) * ROWS] = (
            ((row >> 4) & 1) * 256 + chip * 4 + source * 2 + rank
        )
    tall = dest[...].astype(F32).T.astype(jnp.int32)
    tall_rows = rows[...].astype(F32).T.astype(jnp.int32)
    below = (lane < sub).astype(F32).astype(BF16)
    values = []
    for leaf in range(4):
        mine = tall == myself - z + leaf
        before = jnp.dot(below, mine.astype(F32).astype(BF16), preferred_element_type=F32)
        for slot in range(2):
            hit = mine & (before == slot) & (tall_rows < live - leaf * PR_DEV)
            value = jnp.where(hit, tall_rows + (leaf * PR_DEV + 1), 0)
            values.append(jnp.sum(value, axis=0, keepdims=True))
    values = jnp.concatenate(values, axis=0).astype(F32)

    def spread(count, shift):
        device = lax.broadcasted_iota(jnp.int32, (ROWS, count), 0)
        spot = lax.broadcasted_iota(jnp.int32, (ROWS, count), 1)
        chip = (device >> 5) * 16 + (device & 15)
        owner = (chip == spot >> shift) & ((device >> 4) & 1 == (spot >> 1) & 1)
        owner = owner.astype(F32).astype(BF16)
        total = None
        for term in split3(values):
            part = jnp.dot(term, owner, preferred_element_type=F32)
            total = part if total is None else total + part
        row = lax.broadcasted_iota(jnp.int32, (8, count), 0)
        spot = lax.broadcasted_iota(jnp.int32, (8, count), 1)
        return total, row, spot

    total, row, spot = spread(1024, 4)
    wanted = ((spot >> 2) & 3) * 2 + (spot & 1)
    found = jnp.sum(jnp.where(row == wanted, total, 0.0), axis=0, keepdims=True)
    landing[...] = found.astype(jnp.int32) - 1
    total, row, spot = spread(256, 2)
    found = jnp.sum(jnp.where(row == z * 2 + (spot & 1), total, 0.0), axis=0, keepdims=True)
    found = found.astype(jnp.int32) - 1
    own_landing[...] = jnp.where(found >= 0, found - z * PR_DEV, -1)

    def upright(row):
        return jnp.broadcast_to(row, (K, K)).T

    def take(values, index):
        total = None
        for block, value in enumerate(values):
            part = jnp.where(sub + block * K == index, upright(value), 0.0)
            part = jnp.sum(part, axis=0, keepdims=True)
            total = part if total is None else total + part
        return total

    def order(flag, a, b):
        return jnp.where(flag == 1, b, a), jnp.where(flag == 1, a, b)

    pieces = [line_keys[j].astype(F32)[:1] for j in range(4)]
    pieces = [p[:, :K] * 16.0 + p[:, K:] for p in pieces]
    swapped = order(core, pieces[1], pieces[2])
    by_mask = (pieces[0], swapped[0], pieces[3], swapped[1])
    full = [
        value + ((z ^ mask) * PR_DEV).astype(F32) for mask, value in enumerate(by_mask)
    ]
    odd = z & 1
    pair = order(odd, full[0], full[1])
    far = order(odd, full[2], full[3])
    low = take(pair, merge[pl.ds(grp >> 1, 1), :])
    high = take(far, merge[pl.ds((grp >> 1) ^ 1, 1), :])
    middle = order((z >> 1) & 1, low, high)
    top = take(middle, merge[pl.ds(8 + (grp >> 2), 1), :])
    for block, value in enumerate(pair + middle):
        stack_keys[block * K : (block + 1) * K] = upright(value).astype(jnp.int32)[:, :1]
    top_keys[...] = upright(top).astype(jnp.int32)[:, :1]
    last = merge[pl.ds(12 + (grp >> 3), 1), :].astype(F32)
    chosen[...] = upright(last).astype(jnp.int32)[:, :1]


def pack_kernel(matrix, skeleton, out):
    out[0, :ROWS] = matrix[...]
    value = skeleton[...]
    row = jnp.concatenate([value >> 4, value & 15], axis=1).astype(F32)
    out[0, ROWS:] = jnp.broadcast_to(row, (16, WIDTH)).astype(BF16)


def join_halves_kernel(a, b, left, right, line_keys):
    count = a.shape[0]
    for index, part in enumerate((a, b)):
        rows = slice(index * count, (index + 1) * count)
        left[rows] = part[:, :ROWS, :HALF]
        right[rows] = part[:, :ROWS, HALF:]
        line_keys[rows] = part[:, ROWS:]


def join_halves(a, b):
    half = jax.ShapeDtypeStruct((2 * a.shape[0], ROWS, HALF), a.dtype)
    return call(
        join_halves_kernel,
        (half, half, jax.ShapeDtypeStruct((2 * a.shape[0], 16, WIDTH), a.dtype)),
        (a, b),
        [vmem(), vmem()],
        (vmem(),) * 3,
        limit=3,
    )


def matches(column, row):
    return (column == row).astype(F32).astype(BF16)


def basis_kernel(arrived, landing, keys, out):
    out[...] = jnp.dot(
        matches(keys[...], landing[...]), arrived[...], preferred_element_type=F32
    )


def split2(value):
    hi = value.astype(BF16)
    return hi, (value - hi.astype(F32)).astype(BF16)


def mul(a, b):
    (ah, al), (bh, bl) = split2(a), split2(b)
    wide = jnp.dot(
        jnp.concatenate([ah, al], axis=1),
        jnp.concatenate([bh, bh], axis=0),
        preferred_element_type=F32,
    )
    return wide + jnp.dot(ah, bl, preferred_element_type=F32)


def mul_t(a, b, precision=None):
    dims = (((1,), (1,)), ((), ()))
    if precision is not None:
        return lax.dot_general(a, b, dims, precision=precision, preferred_element_type=F32)
    (ah, al), (bh, bl) = split2(a), split2(b)
    out = None
    for p, q in ((ah, bh), (ah, bl), (al, bh)):
        part = lax.dot_general(p, q, dims, preferred_element_type=F32)
        out = part if out is None else out + part
    return out


def inverses(bases):
    row = lax.broadcasted_iota(jnp.int32, (K, K), 0)
    col = lax.broadcasted_iota(jnp.int32, (K, K), 1)
    ident = (row == col).astype(F32)
    grams = [mul_t(s, s, HIGH) for s in bases]
    state = []
    for index, gram in enumerate(grams):
        trace = jnp.sum(jnp.sum(gram * ident, axis=0, keepdims=True), axis=1, keepdims=True)
        widest = jnp.max(jnp.sum(jnp.abs(gram), axis=0, keepdims=True), axis=1, keepdims=True)
        low = trace * (0.1 / K) + 1e-5
        gram = gram + low * ident
        grams[index] = gram
        high = jnp.maximum(low + jnp.minimum(trace, widest), 2.0 * low)
        scale = 2.0 / (low + high)
        ratio = (high - low) / (high + low)
        residual = ident - scale * gram
        state.append((scale, ratio, residual))
    for index, (scale, ratio, residual) in enumerate(state):
        square = ratio * ratio
        ratio = square / (2.0 - square)
        approx = ((1.0 + ratio) * scale) * (ident + residual)
        residual = (1.0 + ratio) * mul(residual, residual) - ratio * ident
        state[index] = (approx, ratio, residual)
    for step in range(1, DOUBLINGS):
        for index, (approx, ratio, residual) in enumerate(state):
            square = ratio * ratio
            ratio = square / (2.0 - square)
            if step + 1 < DOUBLINGS:
                both = mul(jnp.concatenate([approx, residual], axis=0), residual)
                approx = (1.0 + ratio) * (approx + both[:K])
                residual = (1.0 + ratio) * both[K:] - ratio * ident
            else:
                approx = (1.0 + ratio) * (approx + mul(approx, residual))
            state[index] = (approx, ratio, residual)
    results = []
    for gram, (approx, ratio, residual) in zip(grams, state):
        fix = ident - jnp.dot(gram, approx, precision=HIGH, preferred_element_type=F32)
        results.append((approx, fix))
    return results


def times_inverse(right, approx, fix):
    first = mul(right, approx)
    return first + mul(first, fix)


def choose(flag, first, second):
    return jnp.where(flag == 1, second, first)


def lower_kernel(flags, arrived, landing, own_landing, keys, top, leaf_out, out, built, leaf_rows, sems):
    rows = arrived[...]
    stacks = jnp.dot(matches(keys[...], landing[...]), rows, preferred_element_type=F32)
    first, second = stacks[: 2 * K], stacks[2 * K :]
    leaf = choose(flags[0], first[:K], first[K:])
    node = choose(flags[1], second[:K], second[K:])
    bases = [leaf, node, top[...]]
    row = lax.broadcasted_iota(jnp.int32, (256, 1024), 0)
    col = lax.broadcasted_iota(jnp.int32, (256, 1024), 1)
    spot = (row >> 2) * 16 + flags[3] * 4 + (row & 3)
    mine = jnp.dot(matches(spot, col), rows, preferred_element_type=F32)
    rights = [mul_t(v, s) for v, s in zip((mine, first, second), bases)]
    maps = [times_inverse(r, *pair) for r, pair in zip(rights, inverses(bases))]
    built[...] = jnp.stack(maps[1:])
    copies = [pltpu.make_async_copy(built, out.at[:2], sems.at[4])]
    copies[0].start()
    terms = split2(maps[0])
    for part in range(4):
        spots = lax.broadcasted_iota(jnp.int32, (256, 256), 0) + part * 256
        onehot = matches(spots, own_landing[...])
        leaf_rows[part] = sum(jnp.dot(onehot, t, preferred_element_type=F32) for t in terms)
        copy = pltpu.make_async_copy(
            leaf_rows.at[part], leaf_out.at[0, pl.ds(part * 256, 256)], sems.at[part]
        )
        copy.start()
        copies.append(copy)
    for copy in copies:
        copy.wait()


def upper_kernel(flags, chosen, current, partner, previous, out, top, built, rows, sems):
    mine, other = current[...], partner[...]
    stacked = jnp.concatenate(
        [choose(flags[2], mine, other), choose(flags[2], other, mine)], axis=0
    )
    spots = lax.broadcasted_iota(jnp.int32, (K, 2 * K), 1)
    basis = pick(matches(chosen[...], spots), stacked)
    rows[...] = basis
    early = pltpu.make_async_copy(rows, top, sems.at[0])
    early.start()
    right = mul_t(stacked, basis)
    built[...] = times_inverse(right, *inverses([basis])[0])
    copy = pltpu.make_async_copy(built, out.at[2], sems.at[1])
    copy.start()
    copy.wait()
    early.wait()


def join(a, b, limit):
    return call(
        join_kernel,
        jax.ShapeDtypeStruct((2 * a.shape[0],) + a.shape[1:], a.dtype),
        (a, b),
        [vmem(), vmem()],
        vmem(),
        limit=limit,
    )


def local(contributions, sketch_matrix, destinations, parent_rows, front_sizes, leaf_skeleton, merge_skeleton):
    x, core, grp = lax.axis_index("x"), lax.axis_index("core"), lax.axis_index("grp")
    y, z = grp >> 2, grp & 3
    myself = (x * 2 + core) * 16 + grp
    where = jnp.stack([x, y, z, core]).astype(jnp.int32)

    line = call(
        pack_kernel,
        jax.ShapeDtypeStruct((1, ROWS + 16, WIDTH), BF16),
        (sketch_matrix, leaf_skeleton.reshape(1, K)),
        [vmem(), vmem()],
        vmem(),
        limit=2,
    )
    line = join(line, send(line, route(2, (1, 3))), 2)
    *held, line_keys = join_halves(line, send(line, route(2, (3, 1))))
    one, three = (1, 3), (3, 1)
    for masks in (one, three):
        arriving = [send(held[c], route(ORDERS[c][1], masks)) for c in range(2)]
        held = [join(h, r, 4) for h, r in zip(held, arriving)]
    last = [ORDERS[c][2] for c in range(2)]

    def ring(value, c, masks):
        return send(value, route(last[c], masks))

    nexts = [ring(held[c], c, one) for c in range(2)]
    others = [ring(held[c], c, three) for c in range(2)]
    extra = [ring(nexts[c], c, three) for c in range(2)]
    give = call(
        extract_kernel,
        jax.ShapeDtypeStruct((ROWS, 8192), BF16),
        (where, contributions),
        [smem(), pl.BlockSpec(memory_space=pltpu.HBM)],
        pl.BlockSpec(memory_space=pltpu.HBM),
        [pltpu.VMEM((ROWS, 8192), BF16), pltpu.SemaphoreType.DMA((8,))],
        limit=60,
    )
    received = send(give, core_route())
    place = jnp.stack([myself, core, z, front_sizes[0] - y * 4 * PR_DEV, grp]).astype(jnp.int32)
    column = jax.ShapeDtypeStruct((K, 1), jnp.int32)
    keys, landing, own_landing, stack_keys, top_keys, chosen = call(
        index_kernel,
        tuple(jax.ShapeDtypeStruct((1, n), jnp.int32) for n in (256, 1024, 256))
        + (jax.ShapeDtypeStruct((4 * K, 1), jnp.int32), column, column),
        (
            place,
            destinations.reshape(ROWS, ROWS),
            parent_rows.reshape(ROWS, ROWS),
            line_keys,
            merge_skeleton[0],
        ),
        [smem()] + [vmem()] * 4,
        (vmem(),) * 6,
    )
    flags = jnp.stack([z & 1, (z >> 1) & 1, y & 1, z]).astype(jnp.int32)
    square = jax.ShapeDtypeStruct((256, 256), F32)
    acc, own = call(
        first_kernel,
        (square, jax.ShapeDtypeStruct((ROWS, 8192), BF16)),
        (where, contributions, received, held[0], held[1]),
        [smem(), pl.BlockSpec(memory_space=pltpu.HBM)] + [vmem()] * 3,
        (vmem(), vmem()),
        [pltpu.SemaphoreType.DMA((4,))],
        flops=1 << 28,
        limit=12,
    )
    acc = call(
        middle_kernel,
        square,
        (where, own, received, nexts[0], others[0], nexts[1], others[1], acc),
        [smem()] + [vmem()] * 7,
        vmem(),
        flops=1 << 29,
        limit=12,
    )
    keep, give = call(
        second_kernel,
        (square, square),
        (where, keys, own, received, extra[0], extra[1], acc),
        [smem()] + [vmem()] * 6,
        (vmem(), vmem()),
        flops=1 << 28,
        limit=12,
    )
    packed = call(
        finish_kernel,
        jax.ShapeDtypeStruct((16, 4, 16, WIDTH), BF16),
        (keep, send(give, core_route())),
        [vmem(), vmem()],
        vmem(),
    )
    arrived = lax.all_to_all(
        packed.reshape(64, 16, WIDTH), ("x", "grp"), split_axis=0, concat_axis=0, tiled=True
    ).reshape(1024, WIDTH)

    rows = jax.ShapeDtypeStruct((K, WIDTH), F32)
    current = call(
        basis_kernel, rows, (arrived, landing, top_keys), [vmem()] * 3, vmem(), flops=1 << 24
    )
    partner = send(current, route(1, (1, 1)))
    shape = jax.ShapeDtypeStruct((LEVELS, 2 * K, K), F32)
    leaf_map, maps = call(
        lower_kernel,
        (jax.ShapeDtypeStruct((1, PR_DEV, K), F32), shape),
        (flags, arrived, landing, own_landing, stack_keys, current),
        [smem()] + [vmem()] * 5,
        (hbm(), hbm()),
        [
            pltpu.VMEM((2, 2 * K, K), F32),
            pltpu.VMEM((4, 256, K), F32),
            pltpu.SemaphoreType.DMA((5,)),
        ],
        flops=1 << 31,
        limit=12,
    )
    maps, top = call(
        upper_kernel,
        (shape, rows),
        (flags, chosen, current, partner, maps),
        [smem(), vmem(), vmem(), vmem(), hbm()],
        (hbm(), hbm()),
        [
            pltpu.VMEM((2 * K, K), F32),
            pltpu.VMEM((K, WIDTH), F32),
            pltpu.SemaphoreType.DMA((2,)),
        ],
        flops=1 << 31,
        aliases={4: 0},
    )
    return (leaf_map, maps[None, None], top[None, None])


def solution(mesh):
    inner = Mesh(mesh.devices.reshape(4, 2, 16), ("x", "core", "grp"))
    in_specs = (
        P(ALL, None),
        P(ALL, None),
        P(),
        P(),
        P(("x", "core")),
        P(("x", "core"), "grp", None),
        P(("x", "core"), None, None),
    )
    out_specs = (
        P(("x", "core"), "grp", None),
        P(("x", "core"), "grp", None, None, None),
        P(("x", "core"), "grp", None, None),
    )

    return jax.shard_map(local, mesh=inner, in_specs=in_specs, out_specs=out_specs, check_vma=False)
```

time: 105 us -> 98.2 us (0.935)
  waiting for transfers between devices: 28.4 us -> 34.1 us
  local copies, waits for them, and re-layouts: 8.61 us -> 3.01 us
  starting transfers between devices: 40.9 us -> 35.4 us
    ppermute x17 -> x15, starting transfers between devices: 35.2 us -> 26.9 us  [send(): return lax.ppermute(value, ALL, pairs)]
    ppermute x17 -> x15, waiting for transfers between devices: 16.8 us -> 22.2 us  [send(): return lax.ppermute(value, ALL, pairs)]
    all_to_all x1, starting transfers between devices: 5.76 us -> 8.48 us  [local(): lax.all_to_all(packed.reshape(64, 16, WIDTH), ('x', 'grp'), split_axis=0,...]
    unnamed x15 -> x19, local copies, waits for them, and re-layouts: 5.43 us -> 2.93 us
    pallas_call x1 -> x0, Pallas kernels: 1.98 us -> none  [other_half(): pl.pallas_call(extract_kernel, out_shape=jax.ShapeDtypeStruct((ROWS, 8192...]
    pallas_call x16, Pallas kernels: 21 us -> 22.4 us  [call(): pl.pallas_call(kernel, out_shape=outs, in_specs=specs, out_specs=out_spec...]
    reshape x2 -> x0, local copies, waits for them, and re-layouts: 1.05 us -> none  [the longest x1 0.72 us: local(): chosen = chosen_of(12 + (grp >> 3)).reshape(K, 1)]
  transfers between devices with their start and end apart: 18 -> 16, of which waited for: 11 -> 10; matrix products, arithmetic and copies ran while one was open for 4% -> 0% of each run, Pallas kernels for 13% -> 12%
where the time goes in v2:
time: 98.2 us; the launch traced here: 97.3 us
  starting transfers between devices  35.4 us (36%)
  waiting for transfers between devices  34.1 us (35%)
  Pallas kernels  22.4 us (23%)
  local copies, waits for them, and re-layouts  3.01 us (3%)
  between operations  1.67 us (2%)
    ppermute x15, starting transfers between devices, send(): return lax.ppermute(value, ALL, pairs)  26.9 us
    pallas_call x16, Pallas kernels, call(): pl.pallas_call(kernel, out_shape=outs, in_specs=specs, out_specs=out_spec...  22.4 us
    ppermute x15, waiting for transfers between devices, send(): return lax.ppermute(value, ALL, pairs)  22.2 us
    all_to_all x1, waiting for transfers between devices, local(): lax.all_to_all(packed.reshape(64, 16, WIDTH), ('x', 'grp'), split_axis=0,...  11.9 us
    all_to_all x1, starting transfers between devices, local(): lax.all_to_all(packed.reshape(64, 16, WIDTH), ('x', 'grp'), split_axis=0,...  8.48 us
    unnamed x19, local copies, waits for them, and re-layouts  2.93 us
  transfers between devices with their start and end apart: 16, of which 10 were waited for; matrix products, arithmetic and copies ran while one was open for 0% of the time, Pallas kernels for 12%

profile of v2, /device:TPU:1, one launch (start us, length us, event | category | flops | bytes accessed | tf_op | source)
XLA Modules:
  0.0 97.3 jit_solution(15182561956393988376)
XLA Ops:
  0.6 0.6 pad_add_fusion.1.where
  1.3 3.3 %shard_map.98 = bf16[128,8192]{1,0:T(8,128)(2,1)} custom-call(s32[4]{0:T(128)} %pad_add_fusion.1.where, bf16[128,16384]{1,0:T(8,128)(2,1)} %full.3), custom_call_target="tpu_custom_call" | custom-call | bytes 1048576 | tf_op jit(solution)/shard_map/pallas_call | solution.py:66
  4.6 1.5 %collective-permute-start.2 = (bf16[128,8192]{1,0:T(8,128)(2,1)}, bf16[128,8192]{1,0:T(8,128)(2,1)S(1)}, u32[]{:S(2)}, u32[]{:S(2)}) collective-permute-start(bf16[128,8192]{1,0:T(8,128)(2,1)} %shard_map.98), channel_id=1, source_target_pairs={{0,16},{1,17},{2,18},{3,19},{4,20},{5,21},{6,22},{7,23},{8,24},{9,... | collective-permute-start | bytes 6291464 | tf_op jit(solution)/shard_map/ppermute | solution.py:50
  6.1 3.9 %collective-permute-start = (bf16[1,144,256]{2,1,0:T(8,128)(2,1)S(1)}, bf16[1,144,256]{2,1,0:T(8,128)(2,1)S(1)}, u32[]{:S(2)}, u32[]{:S(2)}) collective-permute-start(bf16[1,144,256]{2,1,0:T(8,128)(2,1)S(1)} %shard_map.94.a), channel_id=1, source_target_pairs={{0,1},{1,0},{2,3},{3,2},{4,5},{5,4},{6,7},{7,6},{8,9},{9,8},{10,11... | collective-permute-start | bytes 221192 | tf_op jit(solution)/shard_map/ppermute | solution.py:50
  10.0 1.7 %collective-permute-done.b = bf16[1,144,256]{2,1,0:T(8,128)(2,1)S(1)} collective-permute-done((bf16[1,144,256]{2,1,0:T(8,128)(2,1)S(1)}, bf16[1,144,256]{2,1,0:T(8,128)(2,1)S(1)}, u32[]{:S(2)}, u32[]{:S(2)}) %collective-permute-start) | collective-permute-done | bytes 73760 | tf_op jit(solution)/shard_map/ppermute | solution.py:50
  11.9 4.3 %collective-permute-done.1.b = bf16[2,144,256]{2,1,0:T(8,128)(2,1)S(1)} collective-permute-done((bf16[2,144,256]{2,1,0:T(8,128)(2,1)S(1)}, bf16[2,144,256]{2,1,0:T(8,128)(2,1)S(1)}, u32[]{:S(2)}, u32[]{:S(2)}) %collective-permute-start.1) | collective-permute-done | bytes 147488 | tf_op jit(solution)/shard_map/ppermute | solution.py:50
  16.2 2.8 %collective-permute-start.5 = (bf16[4,128,128]{2,1,0:T(8,128)(2,1)S(1)}, bf16[4,128,128]{2,1,0:T(8,128)(2,1)S(1)}, u32[]{:S(2)}, u32[]{:S(2)}) collective-permute-start(bf16[4,128,128]{2,1,0:T(8,128)(2,1)S(1)} %get-tuple-element.23.a), channel_id=1, source_target_pairs={{0,4},{1,5},{2,6},{3,7},{4,0},{5,1},{6,2},{7,3},{8,12},{9,13},{10,... | collective-permute-start | bytes 393224 | tf_op jit(solution)/shard_map/ppermute | solution.py:50
  19.0 2.5 %collective-permute-start.3 = (bf16[4,128,128]{2,1,0:T(8,128)(2,1)S(1)}, bf16[4,128,128]{2,1,0:T(8,128)(2,1)S(1)}, u32[]{:S(2)}, u32[]{:S(2)}) collective-permute-start(bf16[4,128,128]{2,1,0:T(8,128)(2,1)S(1)} %get-tuple-element.22.a), channel_id=1, source_target_pairs={{0,32},{1,33},{2,34},{3,35},{4,36},{5,37},{6,38},{7,39},{8,40},{9,... | collective-permute-start | bytes 393224 | tf_op jit(solution)/shard_map/ppermute | solution.py:50
  21.6 2.4 %collective-permute-done.3.b = bf16[4,128,128]{2,1,0:T(8,128)(2,1)S(1)} collective-permute-done((bf16[4,128,128]{2,1,0:T(8,128)(2,1)S(1)}, bf16[4,128,128]{2,1,0:T(8,128)(2,1)S(1)}, u32[]{:S(2)}, u32[]{:S(2)}) %collective-permute-start.3) | collective-permute-done | bytes 131104 | tf_op jit(solution)/shard_map/ppermute | solution.py:50
  24.1 0.4 collective-permute-start.4
  24.4 2.4 %collective-permute-done.6.b = bf16[8,128,128]{2,1,0:T(8,128)(2,1)S(1)} collective-permute-done((bf16[8,128,128]{2,1,0:T(8,128)(2,1)S(1)}, bf16[8,128,128]{2,1,0:T(8,128)(2,1)S(1)}, u32[]{:S(2)}, u32[]{:S(2)}) %collective-permute-start.6) | collective-permute-done | bytes 262176 | tf_op jit(solution)/shard_map/ppermute | solution.py:50
  26.9 2.4 %collective-permute-start.9 = (bf16[16,128,128]{2,1,0:T(8,128)(2,1)S(1)}, bf16[16,128,128]{2,1,0:T(8,128)(2,1)}, u32[]{:S(2)}, u32[]{:S(2)}) collective-permute-start(bf16[16,128,128]{2,1,0:T(8,128)(2,1)S(1)} %shard_map.102.b), channel_id=1, source_target_pairs={{0,32},{1,33},{2,34},{3,35},{4,36},{5,37},{6,38},{7,39},{8,40},{9,... | collective-permute-start | bytes 1572872 | tf_op jit(solution)/shard_map/ppermute | solution.py:50
  29.3 0.4 collective-permute-done.4.b
  29.7 2.4 %collective-permute-start.7 = (bf16[16,128,128]{2,1,0:T(8,128)(2,1)S(1)}, bf16[16,128,128]{2,1,0:T(8,128)(2,1)}, u32[]{:S(2)}, u32[]{:S(2)}) collective-permute-start(bf16[16,128,128]{2,1,0:T(8,128)(2,1)S(1)} %shard_map.100.a), channel_id=1, source_target_pairs={{0,4},{1,5},{2,6},{3,7},{4,0},{5,1},{6,2},{7,3},{8,12},{9,13},{10,... | collective-permute-start | bytes 1572872 | tf_op jit(solution)/shard_map/ppermute | solution.py:50
  32.1 6.7 %collective-permute-done.9.b = bf16[16,128,128]{2,1,0:T(8,128)(2,1)} collective-permute-done((bf16[16,128,128]{2,1,0:T(8,128)(2,1)S(1)}, bf16[16,128,128]{2,1,0:T(8,128)(2,1)}, u32[]{:S(2)}, u32[]{:S(2)}) %collective-permute-start.9) | collective-permute-done | bytes 524320 | tf_op jit(solution)/shard_map/ppermute | solution.py:50
  38.8 0.3 collective-permute-start.10
  39.9 1.2 %shard_map.97 = (s32[1,256]{1,0:T(1,128)S(1)}, s32[1,1024]{1,0:T(1,128)S(1)}, s32[1,256]{1,0:T(1,128)S(1)}, s32[512,1]{1,0:T(8,128)S(1)}, s32[128,1]{1,0:T(8,128)S(1)}, /*index=5*/s32[128,1]{1,0:T(8,128)S(1)}) custom-call(s32[5]{0:T(128)S(1)} %stack.54.place, s32[128,128]{1,0:T(8,128)S(1)} %bitcast.24, s32[128,128]{1,0:T(8,128)S(1)} %bitcast.25, ...), custom_call_target="tpu_custom_call" | custom-call | bytes 1048576 | tf_op jit(solution)/shard_map/pallas_call | solution.py:66
  41.2 0.7 copy-done.6
  41.9 2.2 %copy-done = bf16[128,16384]{1,0:T(8,128)(2,1)S(1)} copy-done((bf16[128,16384]{1,0:T(8,128)(2,1)S(1)}, bf16[128,16384]{1,0:T(8,128)(2,1)}, u32[]{:S(2)}) %copy-start) | copy-done | bytes 4194328
  44.1 1.6 %shard_map.103 = (f32[256,256]{1,0:T(8,128)S(1)}, bf16[128,8192]{1,0:T(8,128)(2,1)S(1)}) custom-call(s32[4]{0:T(128)S(1)} %copy-done.4, bf16[128,16384]{1,0:T(8,128)(2,1)S(1)} %copy-done, bf16[128,8192]{1,0:T(8,128)(2,1)S(1)} %collective-permute-done.2.received, bf16[16,128,128]{2,1,0:T(8,128)(2,1)S(1)} %shard_map.100.a, bf16[16,128,128]{2,1,0:T(8,128)(2,1)S(1)} %shard_map.102.b), custom_call_target="tpu_custom_call" | custom-call | flops 268435456 | bytes 1048576 | tf_op jit(solution)/shard_map/pallas_call | solution.py:66
  45.7 2.9 %shard_map.104.acc = f32[256,256]{1,0:T(8,128)S(1)} custom-call(s32[4]{0:T(128)S(1)} %copy-done.4, bf16[128,8192]{1,0:T(8,128)(2,1)S(1)} %get-tuple-element.24.own, bf16[128,8192]{1,0:T(8,128)(2,1)S(1)} %collective-permute-done.2.received, bf16[16,128,128]{2,1,0:T(8,128)(2,1)} %collective-permute-done.7.a, bf16[16,128,128]{2,1,0:T(8,128)(2,1)} %collective-permute-done.11.c, ...), custom_call_target="tpu_custom_call" | custom-call | flops 536870912 | bytes 1048576 | tf_op jit(solution)/shard_map/pallas_call | solution.py:66
  48.6 2.3 %collective-permute-done.10.b = bf16[16,128,128]{2,1,0:T(8,128)(2,1)} collective-permute-done((bf16[16,128,128]{2,1,0:T(8,128)(2,1)}, bf16[16,128,128]{2,1,0:T(8,128)(2,1)}, u32[]{:S(2)}, u32[]{:S(2)}) %collective-permute-start.10) | collective-permute-done | bytes 524320 | tf_op jit(solution)/shard_map/ppermute | solution.py:50
  50.9 0.8 collective-permute-done.8.a
  51.8 2.3 %shard_map.105 = (f32[256,256]{1,0:T(8,128)S(1)}, f32[256,256]{1,0:T(8,128)S(1)}) custom-call(s32[4]{0:T(128)S(1)} %copy-done.4, s32[1,256]{1,0:T(1,128)S(1)} %get-tuple-element.21.keys, bf16[128,8192]{1,0:T(8,128)(2,1)S(1)} %get-tuple-element.24.own, bf16[128,8192]{1,0:T(8,128)(2,1)S(1)} %collective-permute-done.2.received, ...), custom_call_target="tpu_custom_call" | custom-call | flops 268435456 | bytes 1048576 | tf_op jit(solution)/shard_map/pallas_call | solution.py:66
  54.1 9.5 %collective-permute-start.13 = (f32[256,256]{1,0:T(8,128)S(1)}, f32[256,256]{1,0:T(8,128)S(1)}, u32[]{:S(2)}, u32[]{:S(2)}) collective-permute-start(f32[256,256]{1,0:T(8,128)S(1)} %get-tuple-element.27), channel_id=1, source_target_pairs={{0,16},{1,17},{2,18},{3,19},{4,20},{5,21},{6,22},{7,23},{8,24},{9,... | collective-permute-start | bytes 786440 | tf_op jit(solution)/shard_map/ppermute | solution.py:50
  63.6 1.2 %collective-permute-done.13.given = f32[256,256]{1,0:T(8,128)S(1)} collective-permute-done((f32[256,256]{1,0:T(8,128)S(1)}, f32[256,256]{1,0:T(8,128)S(1)}, u32[]{:S(2)}, u32[]{:S(2)}) %collective-permute-start.13) | collective-permute-done | bytes 262176 | tf_op jit(solution)/shard_map/ppermute | solution.py:50
  64.8 0.8 shard_map.106
  65.6 8.5 %all-to-all-start = ((bf16[64,16,256]{2,1,0:T(8,128)(2,1)}), bf16[64,16,256]{2,1,0:T(8,128)(2,1)S(1)}, u32[]{:S(2)}, u32[]{:S(2)}) async-start(bf16[64,16,256]{2,1,0:T(8,128)(2,1)} %bitcast.14), calls=%async_computation | async-start | bytes 1048576 | tf_op jit(solution)/shard_map/all_to_all | solution.py:549
  74.2 11.9 %all-to-all-done = bf16[64,16,256]{2,1,0:T(8,128)(2,1)S(1)} async-done(((bf16[64,16,256]{2,1,0:T(8,128)(2,1)}), bf16[64,16,256]{2,1,0:T(8,128)(2,1)S(1)}, u32[]{:S(2)}, u32[]{:S(2)}) %all-to-all-start) | async-done | bytes 524320 | tf_op jit(solution)/shard_map/all_to_all | solution.py:549
  86.4 1.0 %collective-permute-start.14 = (f32[128,256]{1,0:T(8,128)S(1)}, f32[128,256]{1,0:T(8,128)S(1)}, u32[]{:S(2)}, u32[]{:S(2)}) collective-permute-start(f32[128,256]{1,0:T(8,128)S(1)} %shard_map.107.top.current), channel_id=1, source_target_pairs={{0,4},{1,5},{2,6},{3,7},{4,0},{5,1},{6,2},{7,3},{8,12},{9,13},{10,... | collective-permute-start | bytes 393224 | tf_op jit(solution)/shard_map/ppermute | solution.py:50
  87.4 5.7 %shard_map.108 = (f32[1,1024,128]{2,1,0:T(8,128)}, f32[3,256,128]{2,1,0:T(8,128)}) custom-call(s32[4]{0:T(128)S(1)} %pad_add_fusion.flags, bf16[1024,256]{1,0:T(8,128)(2,1)S(1)} %bitcast.23, s32[1,1024]{1,0:T(1,128)S(1)} %get-tuple-element.28.landing, s32[1,256]{1,0:T(1,128)S(1)} %get-tuple-element.29.own_landing, s32[512,1]{1,0:T(8,128)S(1)} %copy-done.7, ...), custom_call_target="tpu_custom_call" | custom-call | flops 2147483648 | bytes 1048576 | tf_op jit(solution)/shard_map/pallas_call | solution.py:66
  93.1 4.1 %shard_map.109 = (f32[3,256,128]{2,1,0:T(8,128)}, f32[128,256]{1,0:T(8,128)}) custom-call(s32[4]{0:T(128)S(1)} %pad_add_fusion.flags, s32[128,1]{1,0:T(8,128)S(1)} %get-tuple-element.33.chosen, f32[128,256]{1,0:T(8,128)S(1)} %shard_map.107.top.current, f32[128,256]{1,0:T(8,128)S(1)} %collective-permute-done.14.partner, ...), custom_call_target="tpu_custom_call", output_to_operand_aliasing={{0}: (4, {})} | custom-call | flops 2147483648 | bytes 1048576 | tf_op jit(solution)/shard_map/pallas_call | solution.py:66
  (38 shorter events, 0.9 us)
Async XLA Ops:
  1.3 4.8 %copy-start.1 = (bf16[128,256]{1,0:T(8,128)(2,1)S(1)}, bf16[128,256]{1,0:T(8,128)(2,1)}, u32[]{:S(2)}) copy-start(bf16[128,256]{1,0:T(8,128)(2,1)} %matrix.1) | copy-start | bytes 196612
  1.3 4.8 %copy-start.5 = (s32[1,1,128]{2,1,0:T(1,128)S(1)}, s32[1,1,128]{2,1,0:T(1,128)}, u32[]{:S(2)}) copy-start(s32[1,1,128]{2,1,0:T(1,128)} %param.12) | copy-start | bytes 1540
  4.6 35.3 %copy-start.8 = (s32[1,14,128]{2,0,1:T(1,128)S(1)}, s32[1,14,128]{2,0,1:T(1,128)}, u32[]{:S(2)}) copy-start(s32[1,14,128]{2,0,1:T(1,128)} %param.13) | copy-start | bytes 21508
  4.6 35.4 %copy-start.2 = (s32[16384,1]{0,1:T(1,128)S(1)}, s32[16384,1]{0,1:T(1,128)}, u32[]{:S(2)}) copy-start(s32[16384,1]{0,1:T(1,128)} %param.9) | copy-start | bytes 196612
  4.6 35.3 %copy-start.3 = (s32[16384]{0:T(1024)S(1)}, s32[16384]{0:T(1024)}, u32[]{:S(2)}) copy-start(s32[16384]{0:T(1024)} %param.10) | copy-start | bytes 196612
  4.6 37.3 %copy-start.4 = (s32[4]{0:T(128)S(1)}, s32[4]{0:T(128)}, u32[]{:S(2)}) copy-start(s32[4]{0:T(128)} %pad_add_fusion.1.where) | copy-start | bytes 52
  4.6 37.3 %collective-permute-start.2 = (bf16[128,8192]{1,0:T(8,128)(2,1)}, bf16[128,8192]{1,0:T(8,128)(2,1)S(1)}, u32[]{:S(2)}, u32[]{:S(2)}) collective-permute-start(bf16[128,8192]{1,0:T(8,128)(2,1)} %shard_map.98), channel_id=1, source_target_pairs={{0,16},{1,17},{2,18},{3,19},{4,20},{5,21},{6,22},{7,23},{8,24},{9,... | collective-permute-start | bytes 6291464 | tf_op jit(solution)/shard_map/ppermute | solution.py:50
  6.1 5.7 %collective-permute-start = (bf16[1,144,256]{2,1,0:T(8,128)(2,1)S(1)}, bf16[1,144,256]{2,1,0:T(8,128)(2,1)S(1)}, u32[]{:S(2)}, u32[]{:S(2)}) collective-permute-start(bf16[1,144,256]{2,1,0:T(8,128)(2,1)S(1)} %shard_map.94.a), channel_id=1, source_target_pairs={{0,1},{1,0},{2,3},{3,2},{4,5},{5,4},{6,7},{7,6},{8,9},{9,8},{10,11... | collective-permute-start | bytes 221192 | tf_op jit(solution)/shard_map/ppermute | solution.py:50
  11.8 4.4 %collective-permute-start.1 = (bf16[2,144,256]{2,1,0:T(8,128)(2,1)S(1)}, bf16[2,144,256]{2,1,0:T(8,128)(2,1)S(1)}, u32[]{:S(2)}, u32[]{:S(2)}) collective-permute-start(bf16[2,144,256]{2,1,0:T(8,128)(2,1)S(1)} %shard_map.95.a), channel_id=1, source_target_pairs={{0,3},{1,2},{2,1},{3,0},{4,7},{5,6},{6,5},{7,4},{8,11},{9,10},{10,... | collective-permute-start | bytes 442376 | tf_op jit(solution)/shard_map/ppermute | solution.py:50
  16.2 5.3 %collective-permute-start.5 = (bf16[4,128,128]{2,1,0:T(8,128)(2,1)S(1)}, bf16[4,128,128]{2,1,0:T(8,128)(2,1)S(1)}, u32[]{:S(2)}, u32[]{:S(2)}) collective-permute-start(bf16[4,128,128]{2,1,0:T(8,128)(2,1)S(1)} %get-tuple-element.23.a), channel_id=1, source_target_pairs={{0,4},{1,5},{2,6},{3,7},{4,0},{5,1},{6,2},{7,3},{8,12},{9,13},{10,... | collective-permute-start | bytes 393224 | tf_op jit(solution)/shard_map/ppermute | solution.py:50
  19.0 5.0 %collective-permute-start.3 = (bf16[4,128,128]{2,1,0:T(8,128)(2,1)S(1)}, bf16[4,128,128]{2,1,0:T(8,128)(2,1)S(1)}, u32[]{:S(2)}, u32[]{:S(2)}) collective-permute-start(bf16[4,128,128]{2,1,0:T(8,128)(2,1)S(1)} %get-tuple-element.22.a), channel_id=1, source_target_pairs={{0,32},{1,33},{2,34},{3,35},{4,36},{5,37},{6,38},{7,39},{8,40},{9,... | collective-permute-start | bytes 393224 | tf_op jit(solution)/shard_map/ppermute | solution.py:50
  21.5 5.3 %collective-permute-start.6 = (bf16[8,128,128]{2,1,0:T(8,128)(2,1)S(1)}, bf16[8,128,128]{2,1,0:T(8,128)(2,1)S(1)}, u32[]{:S(2)}, u32[]{:S(2)}) collective-permute-start(bf16[8,128,128]{2,1,0:T(8,128)(2,1)S(1)} %shard_map.101.a), channel_id=1, source_target_pairs={{0,12},{1,13},{2,14},{3,15},{4,8},{5,9},{6,10},{7,11},{8,4},{9,5},... | collective-permute-start | bytes 786440 | tf_op jit(solution)/shard_map/ppermute | solution.py:50
  24.1 5.6 %collective-permute-start.4 = (bf16[8,128,128]{2,1,0:T(8,128)(2,1)S(1)}, bf16[8,128,128]{2,1,0:T(8,128)(2,1)S(1)}, u32[]{:S(2)}, u32[]{:S(2)}) collective-permute-start(bf16[8,128,128]{2,1,0:T(8,128)(2,1)S(1)} %shard_map.99.a), channel_id=1, source_target_pairs={{0,96},{1,97},{2,98},{3,99},{4,100},{5,101},{6,102},{7,103},{8,104... | collective-permute-start | bytes 786440 | tf_op jit(solution)/shard_map/ppermute | solution.py:50
  26.9 12.0 %collective-permute-start.9 = (bf16[16,128,128]{2,1,0:T(8,128)(2,1)S(1)}, bf16[16,128,128]{2,1,0:T(8,128)(2,1)}, u32[]{:S(2)}, u32[]{:S(2)}) collective-permute-start(bf16[16,128,128]{2,1,0:T(8,128)(2,1)S(1)} %shard_map.102.b), channel_id=1, source_target_pairs={{0,32},{1,33},{2,34},{3,35},{4,36},{5,37},{6,38},{7,39},{8,40},{9,... | collective-permute-start | bytes 1572872 | tf_op jit(solution)/shard_map/ppermute | solution.py:50
  29.7 9.4 %collective-permute-start.7 = (bf16[16,128,128]{2,1,0:T(8,128)(2,1)S(1)}, bf16[16,128,128]{2,1,0:T(8,128)(2,1)}, u32[]{:S(2)}, u32[]{:S(2)}) collective-permute-start(bf16[16,128,128]{2,1,0:T(8,128)(2,1)S(1)} %shard_map.100.a), channel_id=1, source_target_pairs={{0,4},{1,5},{2,6},{3,7},{4,0},{5,1},{6,2},{7,3},{8,12},{9,13},{10,... | collective-permute-start | bytes 1572872 | tf_op jit(solution)/shard_map/ppermute | solution.py:50
  32.1 13.6 %collective-permute-start.11 = (bf16[16,128,128]{2,1,0:T(8,128)(2,1)S(1)}, bf16[16,128,128]{2,1,0:T(8,128)(2,1)}, u32[]{:S(2)}, u32[]{:S(2)}) collective-permute-start(bf16[16,128,128]{2,1,0:T(8,128)(2,1)S(1)} %shard_map.100.a), channel_id=1, source_target_pairs={{0,12},{1,13},{2,14},{3,15},{4,8},{5,9},{6,10},{7,11},{8,4},{9,5},... | collective-permute-start | bytes 1572872 | tf_op jit(solution)/shard_map/ppermute | solution.py:50
  32.1 13.6 %collective-permute-start.12 = (bf16[16,128,128]{2,1,0:T(8,128)(2,1)S(1)}, bf16[16,128,128]{2,1,0:T(8,128)(2,1)}, u32[]{:S(2)}, u32[]{:S(2)}) collective-permute-start(bf16[16,128,128]{2,1,0:T(8,128)(2,1)S(1)} %shard_map.102.b), channel_id=1, source_target_pairs={{0,96},{1,97},{2,98},{3,99},{4,100},{5,101},{6,102},{7,103},{8,104... | collective-permute-start | bytes 1572872 | tf_op jit(solution)/shard_map/ppermute | solution.py:50
  38.8 12.1 %collective-permute-start.10 = (bf16[16,128,128]{2,1,0:T(8,128)(2,1)}, bf16[16,128,128]{2,1,0:T(8,128)(2,1)}, u32[]{:S(2)}, u32[]{:S(2)}) collective-permute-start(bf16[16,128,128]{2,1,0:T(8,128)(2,1)} %collective-permute-done.9.b), channel_id=1, source_target_pairs={{0,96},{1,97},{2,98},{3,99},{4,100},{5,101},{6,102},{7,103},{8,104... | collective-permute-start | bytes 1572872 | tf_op jit(solution)/shard_map/ppermute | solution.py:50
  39.1 12.6 %collective-permute-start.8 = (bf16[16,128,128]{2,1,0:T(8,128)(2,1)}, bf16[16,128,128]{2,1,0:T(8,128)(2,1)}, u32[]{:S(2)}, u32[]{:S(2)}) collective-permute-start(bf16[16,128,128]{2,1,0:T(8,128)(2,1)} %collective-permute-done.7.a), channel_id=1, source_target_pairs={{0,12},{1,13},{2,14},{3,15},{4,8},{5,9},{6,10},{7,11},{8,4},{9,5},... | collective-permute-start | bytes 1572872 | tf_op jit(solution)/shard_map/ppermute | solution.py:50
  41.2 0.7 copy-start.6
  41.9 2.2 %copy-start = (bf16[128,16384]{1,0:T(8,128)(2,1)S(1)}, bf16[128,16384]{1,0:T(8,128)(2,1)}, u32[]{:S(2)}) copy-start(bf16[128,16384]{1,0:T(8,128)(2,1)} %full.3) | copy-start | bytes 12582916
  54.1 33.3 %copy-start.7 = (s32[512,1]{1,0:T(8,128)S(1)}, s32[512,1]{1,0:T(8,128)}, u32[]{:S(2)}) copy-start(s32[512,1]{1,0:T(8,128)} %copy-done.6) | copy-start | bytes 6148
  54.1 10.7 %collective-permute-start.13 = (f32[256,256]{1,0:T(8,128)S(1)}, f32[256,256]{1,0:T(8,128)S(1)}, u32[]{:S(2)}, u32[]{:S(2)}) collective-permute-start(f32[256,256]{1,0:T(8,128)S(1)} %get-tuple-element.27), channel_id=1, source_target_pairs={{0,16},{1,17},{2,18},{3,19},{4,20},{5,21},{6,22},{7,23},{8,24},{9,... | collective-permute-start | bytes 786440 | tf_op jit(solution)/shard_map/ppermute | solution.py:50
  65.6 20.5 %all-to-all-start = ((bf16[64,16,256]{2,1,0:T(8,128)(2,1)}), bf16[64,16,256]{2,1,0:T(8,128)(2,1)S(1)}, u32[]{:S(2)}, u32[]{:S(2)}) async-start(bf16[64,16,256]{2,1,0:T(8,128)(2,1)} %bitcast.14), calls=%async_computation | async-start | bytes 1048576 | tf_op jit(solution)/shard_map/all_to_all | solution.py:549
  86.4 6.7 %collective-permute-start.14 = (f32[128,256]{1,0:T(8,128)S(1)}, f32[128,256]{1,0:T(8,128)S(1)}, u32[]{:S(2)}, u32[]{:S(2)}) collective-permute-start(f32[128,256]{1,0:T(8,128)S(1)} %shard_map.107.top.current), channel_id=1, source_target_pairs={{0,4},{1,5},{2,6},{3,7},{4,0},{5,1},{6,2},{7,3},{8,12},{9,13},{10,... | collective-permute-start | bytes 393224 | tf_op jit(solution)/shard_map/ppermute | solution.py:50

commit v3 on v2

--- a/solution.py
+++ b/solution.py
@@ -246,9 +246,6 @@
     found = found.astype(jnp.int32) - 1
     own_landing[...] = jnp.where(found >= 0, found - z * PR_DEV, -1)
 
-    def upright(row):
-        return jnp.broadcast_to(row, (K, K)).T
-
     def take(values, index):
         total = None
         for block, value in enumerate(values):
@@ -274,16 +271,26 @@
     high = take(far, merge[pl.ds((grp >> 1) ^ 1, 1), :])
     middle = order((z >> 1) & 1, low, high)
     top = take(middle, merge[pl.ds(8 + (grp >> 2), 1), :])
-    for block, value in enumerate(pair + middle):
-        stack_keys[block * K : (block + 1) * K] = upright(value).astype(jnp.int32)[:, :1]
+    stack_keys[...] = jnp.concatenate(pair + middle, axis=0).astype(jnp.int32)
     top_keys[...] = upright(top).astype(jnp.int32)[:, :1]
     last = merge[pl.ds(12 + (grp >> 3), 1), :].astype(F32)
     chosen[...] = upright(last).astype(jnp.int32)[:, :1]
 
 
-def pack_kernel(matrix, skeleton, out):
-    out[0, :ROWS] = matrix[...]
-    value = skeleton[...]
+def upright(row):
+    return jnp.broadcast_to(row, (K, K)).T
+
+
+def pack_kernel(matrix, skeleton, out, index, sems):
+    copies = [
+        pltpu.make_async_copy(matrix, out.at[0, :ROWS], sems.at[0]),
+        pltpu.make_async_copy(skeleton, index, sems.at[1]),
+    ]
+    for copy in copies:
+        copy.start()
+    for copy in copies:
+        copy.wait()
+    value = index[...]
     row = jnp.concatenate([value >> 4, value & 15], axis=1).astype(F32)
     out[0, ROWS:] = jnp.broadcast_to(row, (16, WIDTH)).astype(BF16)
 
@@ -396,9 +403,12 @@
     return jnp.where(flag == 1, second, first)
 
 
-def lower_kernel(flags, arrived, landing, own_landing, keys, top, leaf_out, out, built, leaf_rows, sems):
+def lower_kernel(flags, arrived, landing, keys, top, leaf_rows, out, built, sem):
     rows = arrived[...]
-    stacks = jnp.dot(matches(keys[...], landing[...]), rows, preferred_element_type=F32)
+    tall = keys[...].astype(F32)
+    tall = [upright(tall[j : j + 1])[:, :1] for j in range(4)]
+    tall = jnp.concatenate(tall, axis=0).astype(jnp.int32)
+    stacks = jnp.dot(matches(tall, landing[...]), rows, preferred_element_type=F32)
     first, second = stacks[: 2 * K], stacks[2 * K :]
     leaf = choose(flags[0], first[:K], first[K:])
     node = choose(flags[1], second[:K], second[K:])
@@ -410,38 +420,54 @@
     rights = [mul_t(v, s) for v, s in zip((mine, first, second), bases)]
     maps = [times_inverse(r, *pair) for r, pair in zip(rights, inverses(bases))]
     built[...] = jnp.stack(maps[1:])
-    copies = [pltpu.make_async_copy(built, out.at[:2], sems.at[4])]
+    copy = pltpu.make_async_copy(built, out.at[:2], sem)
+    copy.start()
+    leaf_rows[...] = maps[0]
+    copy.wait()
+
+
+def upper_kernel(
+    flags,
+    chosen,
+    current,
+    partner,
+    own_landing,
+    leaf,
+    previous,
+    leaf_out,
+    out,
+    top,
+    built,
+    rows,
+    blocks,
+    sems,
+):
+    mine, other = current[...], partner[...]
+    stacked = jnp.concatenate(
+        [choose(flags[2], mine, other), choose(flags[2], other, mine)], axis=0
+    )
+    spots = lax.broadcasted_iota(jnp.int32, (K, 2 * K), 1)
+    basis = pick(matches(chosen[...], spots), stacked)
+    rows[...] = basis
+    copies = [pltpu.make_async_copy(rows, top, sems.at[0])]
     copies[0].start()
-    terms = split2(maps[0])
+    terms = split2(leaf[...])
     for part in range(4):
         spots = lax.broadcasted_iota(jnp.int32, (256, 256), 0) + part * 256
         onehot = matches(spots, own_landing[...])
-        leaf_rows[part] = sum(jnp.dot(onehot, t, preferred_element_type=F32) for t in terms)
-        copy = pltpu.make_async_copy(
-            leaf_rows.at[part], leaf_out.at[0, pl.ds(part * 256, 256)], sems.at[part]
+        blocks[part] = sum(jnp.dot(onehot, t, preferred_element_type=F32) for t in terms)
+        copies.append(
+            pltpu.make_async_copy(
+                blocks.at[part], leaf_out.at[0, pl.ds(part * 256, 256)], sems.at[2 + part]
+            )
         )
-        copy.start()
-        copies.append(copy)
+        copies[-1].start()
+    right = mul_t(stacked, basis)
+    built[...] = times_inverse(right, *inverses([basis])[0])
+    copies.append(pltpu.make_async_copy(built, out.at[2], sems.at[1]))
+    copies[-1].start()
     for copy in copies:
         copy.wait()
-
-
-def upper_kernel(flags, chosen, current, partner, previous, out, top, built, rows, sems):
-    mine, other = current[...], partner[...]
-    stacked = jnp.concatenate(
-        [choose(flags[2], mine, other), choose(flags[2], other, mine)], axis=0
-    )
-    spots = lax.broadcasted_iota(jnp.int32, (K, 2 * K), 1)
-    basis = pick(matches(chosen[...], spots), stacked)
-    rows[...] = basis
-    early = pltpu.make_async_copy(rows, top, sems.at[0])
-    early.start()
-    right = mul_t(stacked, basis)
-    built[...] = times_inverse(right, *inverses([basis])[0])
-    copy = pltpu.make_async_copy(built, out.at[2], sems.at[1])
-    copy.start()
-    copy.wait()
-    early.wait()
 
 
 def join(a, b, limit):
@@ -464,9 +490,13 @@
     line = call(
         pack_kernel,
         jax.ShapeDtypeStruct((1, ROWS + 16, WIDTH), BF16),
-        (sketch_matrix, leaf_skeleton.reshape(1, K)),
-        [vmem(), vmem()],
+        tuple(
+            pltpu.with_memory_space_constraint(value, pltpu.HBM)
+            for value in (sketch_matrix, leaf_skeleton.reshape(1, K))
+        ),
+        [pl.BlockSpec(memory_space=pltpu.HBM)] * 2,
         vmem(),
+        [pltpu.VMEM((1, K), jnp.int32), pltpu.SemaphoreType.DMA((2,))],
         limit=2,
     )
     line = join(line, send(line, route(2, (1, 3))), 2)
@@ -486,11 +516,11 @@
     give = call(
         extract_kernel,
         jax.ShapeDtypeStruct((ROWS, 8192), BF16),
-        (where, contributions),
+        (where, pltpu.with_memory_space_constraint(contributions, pltpu.HBM)),
         [smem(), pl.BlockSpec(memory_space=pltpu.HBM)],
         pl.BlockSpec(memory_space=pltpu.HBM),
         [pltpu.VMEM((ROWS, 8192), BF16), pltpu.SemaphoreType.DMA((8,))],
-        limit=60,
+        limit=6,
     )
     received = send(give, core_route())
     place = jnp.stack([myself, core, z, front_sizes[0] - y * 4 * PR_DEV, grp]).astype(jnp.int32)
@@ -498,7 +528,7 @@
     keys, landing, own_landing, stack_keys, top_keys, chosen = call(
         index_kernel,
         tuple(jax.ShapeDtypeStruct((1, n), jnp.int32) for n in (256, 1024, 256))
-        + (jax.ShapeDtypeStruct((4 * K, 1), jnp.int32), column, column),
+        + (jax.ShapeDtypeStruct((4, K), jnp.int32), column, column),
         (
             place,
             destinations.reshape(ROWS, ROWS),
@@ -514,7 +544,13 @@
     acc, own = call(
         first_kernel,
         (square, jax.ShapeDtypeStruct((ROWS, 8192), BF16)),
-        (where, contributions, received, held[0], held[1]),
+        (
+            where,
+            pltpu.with_memory_space_constraint(contributions, pltpu.HBM),
+            received,
+            held[0],
+            held[1],
+        ),
         [smem(), pl.BlockSpec(memory_space=pltpu.HBM)] + [vmem()] * 3,
         (vmem(), vmem()),
         [pltpu.SemaphoreType.DMA((4,))],
@@ -556,33 +592,30 @@
     )
     partner = send(current, route(1, (1, 1)))
     shape = jax.ShapeDtypeStruct((LEVELS, 2 * K, K), F32)
-    leaf_map, maps = call(
+    leaf, maps = call(
         lower_kernel,
-        (jax.ShapeDtypeStruct((1, PR_DEV, K), F32), shape),
-        (flags, arrived, landing, own_landing, stack_keys, current),
-        [smem()] + [vmem()] * 5,
-        (hbm(), hbm()),
-        [
-            pltpu.VMEM((2, 2 * K, K), F32),
-            pltpu.VMEM((4, 256, K), F32),
-            pltpu.SemaphoreType.DMA((5,)),
-        ],
+        (jax.ShapeDtypeStruct((2 * K, K), F32), shape),
+        (flags, arrived, landing, stack_keys, current),
+        [smem()] + [vmem()] * 4,
+        (vmem(), hbm()),
+        [pltpu.VMEM((2, 2 * K, K), F32), pltpu.SemaphoreType.DMA],
         flops=1 << 31,
         limit=12,
     )
-    maps, top = call(
+    leaf_map, maps, top = call(
         upper_kernel,
-        (shape, rows),
-        (flags, chosen, current, partner, maps),
-        [smem(), vmem(), vmem(), vmem(), hbm()],
-        (hbm(), hbm()),
+        (jax.ShapeDtypeStruct((1, PR_DEV, K), F32), shape, rows),
+        (flags, chosen, current, partner, own_landing, leaf, maps),
+        [smem()] + [vmem()] * 5 + [hbm()],
+        (hbm(),) * 3,
         [
             pltpu.VMEM((2 * K, K), F32),
             pltpu.VMEM((K, WIDTH), F32),
-            pltpu.SemaphoreType.DMA((2,)),
+            pltpu.VMEM((4, 256, K), F32),
+            pltpu.SemaphoreType.DMA((6,)),
         ],
         flops=1 << 31,
-        aliases={4: 0},
+        aliases={6: 1},
     )
     return (leaf_map, maps[None, None], top[None, None])
 

time: 98.2 us -> 96.7 us (0.985)
  local copies, waits for them, and re-layouts: 3.01 us -> 0.11 us
  Pallas kernels: 22.4 us -> 24.3 us
  waiting for transfers between devices: 34.1 us -> 35.8 us
  starting transfers between devices: 35.4 us -> 33.9 us
    unnamed x19 -> x7, local copies, waits for them, and re-layouts: 2.93 us -> 0.02 us
    pallas_call x16, Pallas kernels: 22.4 us -> 24.3 us  [call(): pl.pallas_call(kernel, out_shape=outs, in_specs=specs, out_specs=out_spec...]
    ppermute x15, waiting for transfers between devices: 22.2 us -> 23.9 us  [send(): return lax.ppermute(value, ALL, pairs)]
    all_to_all x1, starting transfers between devices: 8.48 us -> 6.95 us  [local(): lax.all_to_all(packed.reshape(64, 16, WIDTH), ('x', 'grp'), split_axis=0,...]
  transfers between devices with their start and end apart: 16 -> 16, of which waited for: 10 -> 11; matrix products, arithmetic and copies ran while one was open for 0% -> 0% of each run, Pallas kernels for 12% -> 14%
where the time goes in v3:
time: 96.7 us; the launch traced here: 95.9 us
  waiting for transfers between devices  35.8 us (37%)
  starting transfers between devices  33.9 us (35%)
  Pallas kernels  24.3 us (25%)
  between operations  1.65 us (2%)
    ppermute x15, starting transfers between devices, send(): return lax.ppermute(value, ALL, pairs)  26.9 us
    pallas_call x16, Pallas kernels, call(): pl.pallas_call(kernel, out_shape=outs, in_specs=specs, out_specs=out_spec...  24.3 us
    ppermute x15, waiting for transfers between devices, send(): return lax.ppermute(value, ALL, pairs)  23.9 us
    all_to_all x1, waiting for transfers between devices, local(): lax.all_to_all(packed.reshape(64, 16, WIDTH), ('x', 'grp'), split_axis=0,...  11.9 us
    all_to_all x1, starting transfers between devices, local(): lax.all_to_all(packed.reshape(64, 16, WIDTH), ('x', 'grp'), split_axis=0,...  6.95 us
  transfers between devices with their start and end apart: 16, of which 11 were waited for; matrix products, arithmetic and copies ran while one was open for 0% of the time, Pallas kernels for 14%

profile of v3, /device:TPU:1, one launch (start us, length us, event | category | flops | bytes accessed | tf_op | source)
XLA Modules:
  0.0 95.9 jit_solution(17627898357748610212)
XLA Ops:
  0.7 3.0 %shard_map.98 = bf16[128,8192]{1,0:T(8,128)(2,1)} custom-call(s32[4]{0:T(128)S(1)} %pad_add_fusion.1.where, bf16[128,16384]{1,0:T(8,128)(2,1)} %full.3), custom_call_target="tpu_custom_call" | custom-call | bytes 1048576 | tf_op jit(solution)/shard_map/pallas_call | solution.py:66
  3.7 1.5 %collective-permute-start.2 = (bf16[128,8192]{1,0:T(8,128)(2,1)}, bf16[128,8192]{1,0:T(8,128)(2,1)S(1)}, u32[]{:S(2)}, u32[]{:S(2)}) collective-permute-start(bf16[128,8192]{1,0:T(8,128)(2,1)} %shard_map.98), channel_id=1, source_target_pairs={{0,16},{1,17},{2,18},{3,19},{4,20},{5,21},{6,22},{7,23},{8,24},{9,... | collective-permute-start | bytes 6291464 | tf_op jit(solution)/shard_map/ppermute | solution.py:50
  5.2 0.9 shard_map.94.a
  6.1 3.9 %collective-permute-start = (bf16[1,144,256]{2,1,0:T(8,128)(2,1)S(1)}, bf16[1,144,256]{2,1,0:T(8,128)(2,1)S(1)}, u32[]{:S(2)}, u32[]{:S(2)}) collective-permute-start(bf16[1,144,256]{2,1,0:T(8,128)(2,1)S(1)} %shard_map.94.a), channel_id=1, source_target_pairs={{0,1},{1,0},{2,3},{3,2},{4,5},{5,4},{6,7},{7,6},{8,9},{9,8},{10,11... | collective-permute-start | bytes 221192 | tf_op jit(solution)/shard_map/ppermute | solution.py:50
  10.0 1.7 %collective-permute-done.b = bf16[1,144,256]{2,1,0:T(8,128)(2,1)S(1)} collective-permute-done((bf16[1,144,256]{2,1,0:T(8,128)(2,1)S(1)}, bf16[1,144,256]{2,1,0:T(8,128)(2,1)S(1)}, u32[]{:S(2)}, u32[]{:S(2)}) %collective-permute-start) | collective-permute-done | bytes 73760 | tf_op jit(solution)/shard_map/ppermute | solution.py:50
  11.9 4.3 %collective-permute-done.1.b = bf16[2,144,256]{2,1,0:T(8,128)(2,1)S(1)} collective-permute-done((bf16[2,144,256]{2,1,0:T(8,128)(2,1)S(1)}, bf16[2,144,256]{2,1,0:T(8,128)(2,1)S(1)}, u32[]{:S(2)}, u32[]{:S(2)}) %collective-permute-start.1) | collective-permute-done | bytes 147488 | tf_op jit(solution)/shard_map/ppermute | solution.py:50
  16.2 2.8 %collective-permute-start.5 = (bf16[4,128,128]{2,1,0:T(8,128)(2,1)S(1)}, bf16[4,128,128]{2,1,0:T(8,128)(2,1)S(1)}, u32[]{:S(2)}, u32[]{:S(2)}) collective-permute-start(bf16[4,128,128]{2,1,0:T(8,128)(2,1)S(1)} %get-tuple-element.25.a), channel_id=1, source_target_pairs={{0,4},{1,5},{2,6},{3,7},{4,0},{5,1},{6,2},{7,3},{8,12},{9,13},{10,... | collective-permute-start | bytes 393224 | tf_op jit(solution)/shard_map/ppermute | solution.py:50
  19.0 2.5 %collective-permute-start.3 = (bf16[4,128,128]{2,1,0:T(8,128)(2,1)S(1)}, bf16[4,128,128]{2,1,0:T(8,128)(2,1)S(1)}, u32[]{:S(2)}, u32[]{:S(2)}) collective-permute-start(bf16[4,128,128]{2,1,0:T(8,128)(2,1)S(1)} %get-tuple-element.24.a), channel_id=1, source_target_pairs={{0,32},{1,33},{2,34},{3,35},{4,36},{5,37},{6,38},{7,39},{8,40},{9,... | collective-permute-start | bytes 393224 | tf_op jit(solution)/shard_map/ppermute | solution.py:50
  21.6 2.4 %collective-permute-done.3.b = bf16[4,128,128]{2,1,0:T(8,128)(2,1)S(1)} collective-permute-done((bf16[4,128,128]{2,1,0:T(8,128)(2,1)S(1)}, bf16[4,128,128]{2,1,0:T(8,128)(2,1)S(1)}, u32[]{:S(2)}, u32[]{:S(2)}) %collective-permute-start.3) | collective-permute-done | bytes 131104 | tf_op jit(solution)/shard_map/ppermute | solution.py:50
  24.1 0.4 collective-permute-start.4
  24.4 2.4 %collective-permute-done.6.b = bf16[8,128,128]{2,1,0:T(8,128)(2,1)S(1)} collective-permute-done((bf16[8,128,128]{2,1,0:T(8,128)(2,1)S(1)}, bf16[8,128,128]{2,1,0:T(8,128)(2,1)S(1)}, u32[]{:S(2)}, u32[]{:S(2)}) %collective-permute-start.6) | collective-permute-done | bytes 262176 | tf_op jit(solution)/shard_map/ppermute | solution.py:50
  26.9 2.4 %collective-permute-start.9 = (bf16[16,128,128]{2,1,0:T(8,128)(2,1)S(1)}, bf16[16,128,128]{2,1,0:T(8,128)(2,1)}, u32[]{:S(2)}, u32[]{:S(2)}) collective-permute-start(bf16[16,128,128]{2,1,0:T(8,128)(2,1)S(1)} %shard_map.102.b), channel_id=1, source_target_pairs={{0,32},{1,33},{2,34},{3,35},{4,36},{5,37},{6,38},{7,39},{8,40},{9,... | collective-permute-start | bytes 1572872 | tf_op jit(solution)/shard_map/ppermute | solution.py:50
  29.3 0.4 collective-permute-done.4.b
  29.7 2.4 %collective-permute-start.7 = (bf16[16,128,128]{2,1,0:T(8,128)(2,1)S(1)}, bf16[16,128,128]{2,1,0:T(8,128)(2,1)}, u32[]{:S(2)}, u32[]{:S(2)}) collective-permute-start(bf16[16,128,128]{2,1,0:T(8,128)(2,1)S(1)} %shard_map.100.a), channel_id=1, source_target_pairs={{0,4},{1,5},{2,6},{3,7},{4,0},{5,1},{6,2},{7,3},{8,12},{9,13},{10,... | collective-permute-start | bytes 1572872 | tf_op jit(solution)/shard_map/ppermute | solution.py:50
  32.1 6.7 %collective-permute-done.9.b = bf16[16,128,128]{2,1,0:T(8,128)(2,1)} collective-permute-done((bf16[16,128,128]{2,1,0:T(8,128)(2,1)S(1)}, bf16[16,128,128]{2,1,0:T(8,128)(2,1)}, u32[]{:S(2)}, u32[]{:S(2)}) %collective-permute-start.9) | collective-permute-done | bytes 524320 | tf_op jit(solution)/shard_map/ppermute | solution.py:50
  38.8 0.3 collective-permute-start.10
  39.9 1.2 %shard_map.97 = (s32[1,256]{1,0:T(1,128)S(1)}, s32[1,1024]{1,0:T(1,128)S(1)}, s32[1,256]{1,0:T(1,128)S(1)}, s32[4,128]{1,0:T(4,128)S(1)}, s32[128,1]{1,0:T(8,128)S(1)}, /*index=5*/s32[128,1]{1,0:T(8,128)S(1)}) custom-call(s32[5]{0:T(128)S(1)} %stack.51.place, s32[128,128]{1,0:T(8,128)S(1)} %bitcast.24, s32[128,128]{1,0:T(8,128)S(1)} %bitcast.25, ...), custom_call_target="tpu_custom_call" | custom-call | bytes 1048576 | tf_op jit(solution)/shard_map/pallas_call | solution.py:66
  41.2 2.9 %shard_map.103 = (f32[256,256]{1,0:T(8,128)S(1)}, bf16[128,8192]{1,0:T(8,128)(2,1)S(1)}) custom-call(s32[4]{0:T(128)S(1)} %pad_add_fusion.1.where, bf16[128,16384]{1,0:T(8,128)(2,1)} %full.3, bf16[128,8192]{1,0:T(8,128)(2,1)S(1)} %collective-permute-done.2.received, bf16[16,128,128]{2,1,0:T(8,128)(2,1)S(1)} %shard_map.100.a, ...), custom_call_target="tpu_custom_call" | custom-call | flops 268435456 | bytes 1048576 | tf_op jit(solution)/shard_map/pallas_call | solution.py:66
  44.1 1.2 %collective-permute-done.12.d = bf16[16,128,128]{2,1,0:T(8,128)(2,1)} collective-permute-done((bf16[16,128,128]{2,1,0:T(8,128)(2,1)S(1)}, bf16[16,128,128]{2,1,0:T(8,128)(2,1)}, u32[]{:S(2)}, u32[]{:S(2)}) %collective-permute-start.12) | collective-permute-done | bytes 524320 | tf_op jit(solution)/shard_map/ppermute | solution.py:50
  45.3 2.9 %shard_map.104.acc = f32[256,256]{1,0:T(8,128)S(1)} custom-call(s32[4]{0:T(128)S(1)} %pad_add_fusion.1.where, bf16[128,8192]{1,0:T(8,128)(2,1)S(1)} %get-tuple-element.26.own, bf16[128,8192]{1,0:T(8,128)(2,1)S(1)} %collective-permute-done.2.received, bf16[16,128,128]{2,1,0:T(8,128)(2,1)} %collective-permute-done.7.a, ...), custom_call_target="tpu_custom_call" | custom-call | flops 536870912 | bytes 1048576 | tf_op jit(solution)/shard_map/pallas_call | solution.py:66
  48.2 2.7 %collective-permute-done.10.b = bf16[16,128,128]{2,1,0:T(8,128)(2,1)} collective-permute-done((bf16[16,128,128]{2,1,0:T(8,128)(2,1)}, bf16[16,128,128]{2,1,0:T(8,128)(2,1)}, u32[]{:S(2)}, u32[]{:S(2)}) %collective-permute-start.10) | collective-permute-done | bytes 524320 | tf_op jit(solution)/shard_map/ppermute | solution.py:50
  50.9 0.8 collective-permute-done.8.a
  51.8 2.3 %shard_map.105 = (f32[256,256]{1,0:T(8,128)S(1)}, f32[256,256]{1,0:T(8,128)S(1)}) custom-call(s32[4]{0:T(128)S(1)} %pad_add_fusion.1.where, s32[1,256]{1,0:T(1,128)S(1)} %get-tuple-element.23.keys, bf16[128,8192]{1,0:T(8,128)(2,1)S(1)} %get-tuple-element.26.own, bf16[128,8192]{1,0:T(8,128)(2,1)S(1)} %collective-permute-done.2.received, ...), custom_call_target="tpu_custom_call" | custom-call | flops 268435456 | bytes 1048576 | tf_op jit(solution)/shard_map/pallas_call | solution.py:66
  54.1 9.6 %collective-permute-start.13 = (f32[256,256]{1,0:T(8,128)S(1)}, f32[256,256]{1,0:T(8,128)S(1)}, u32[]{:S(2)}, u32[]{:S(2)}) collective-permute-start(f32[256,256]{1,0:T(8,128)S(1)} %get-tuple-element.29), channel_id=1, source_target_pairs={{0,16},{1,17},{2,18},{3,19},{4,20},{5,21},{6,22},{7,23},{8,24},{9,... | collective-permute-start | bytes 786440 | tf_op jit(solution)/shard_map/ppermute | solution.py:50
  63.6 1.2 %collective-permute-done.13.given = f32[256,256]{1,0:T(8,128)S(1)} collective-permute-done((f32[256,256]{1,0:T(8,128)S(1)}, f32[256,256]{1,0:T(8,128)S(1)}, u32[]{:S(2)}, u32[]{:S(2)}) %collective-permute-start.13) | collective-permute-done | bytes 262176 | tf_op jit(solution)/shard_map/ppermute | solution.py:50
  64.8 0.8 shard_map.106
  65.6 7.0 %all-to-all-start = ((bf16[64,16,256]{2,1,0:T(8,128)(2,1)}), bf16[64,16,256]{2,1,0:T(8,128)(2,1)S(1)}, u32[]{:S(2)}, u32[]{:S(2)}) async-start(bf16[64,16,256]{2,1,0:T(8,128)(2,1)} %bitcast.14), calls=%async_computation | async-start | bytes 1048576 | tf_op jit(solution)/shard_map/all_to_all | solution.py:585
  72.7 11.9 %all-to-all-done = bf16[64,16,256]{2,1,0:T(8,128)(2,1)S(1)} async-done(((bf16[64,16,256]{2,1,0:T(8,128)(2,1)}), bf16[64,16,256]{2,1,0:T(8,128)(2,1)S(1)}, u32[]{:S(2)}, u32[]{:S(2)}) %all-to-all-start) | async-done | bytes 524320 | tf_op jit(solution)/shard_map/all_to_all | solution.py:585
  84.6 0.3 shard_map.107.top.current
  84.8 1.0 %collective-permute-start.14 = (f32[128,256]{1,0:T(8,128)S(1)}, f32[128,256]{1,0:T(8,128)S(1)}, u32[]{:S(2)}, u32[]{:S(2)}) collective-permute-start(f32[128,256]{1,0:T(8,128)S(1)} %shard_map.107.top.current), channel_id=1, source_target_pairs={{0,4},{1,5},{2,6},{3,7},{4,0},{5,1},{6,2},{7,3},{8,12},{9,13},{10,... | collective-permute-start | bytes 393224 | tf_op jit(solution)/shard_map/ppermute | solution.py:50
  85.8 5.7 %shard_map.108 = (f32[256,128]{1,0:T(8,128)S(1)}, f32[3,256,128]{2,1,0:T(8,128)}) custom-call(s32[4]{0:T(128)S(1)} %pad_add_fusion.flags, bf16[1024,256]{1,0:T(8,128)(2,1)S(1)} %bitcast.23, s32[1,1024]{1,0:T(1,128)S(1)} %get-tuple-element.30.landing, s32[4,128]{1,0:T(4,128)S(1)} %get-tuple-element.33.keys, f32[128,256]{1,0:T(8,128)S(1)} %shard_map.107.top.current), custom_call_target="tpu_custom_call" | custom-call | flops 2147483648 | bytes 1048576 | tf_op jit(solution)/shard_map/pallas_call | solution.py:66
  91.5 4.2 %shard_map.109 = (f32[1,1024,128]{2,1,0:T(8,128)}, f32[3,256,128]{2,1,0:T(8,128)}, f32[128,256]{1,0:T(8,128)}) custom-call(s32[4]{0:T(128)S(1)} %pad_add_fusion.flags, s32[128,1]{1,0:T(8,128)S(1)} %get-tuple-element.22.chosen, f32[128,256]{1,0:T(8,128)S(1)} %shard_map.107.top.current, ...), custom_call_target="tpu_custom_call", output_to_operand_aliasing={{1}: (6, {})} | custom-call | flops 2147483648 | bytes 1048576 | tf_op jit(solution)/shard_map/pallas_call | solution.py:66
  (26 shorter events, 0.6 us)
Async XLA Ops:
  3.7 36.1 %copy-start.2 = (s32[1,14,128]{2,0,1:T(1,128)S(1)}, s32[1,14,128]{2,0,1:T(1,128)}, u32[]{:S(2)}) copy-start(s32[1,14,128]{2,0,1:T(1,128)} %param.13) | copy-start | bytes 21508
  3.7 36.2 %copy-start = (s32[16384,1]{0,1:T(1,128)S(1)}, s32[16384,1]{0,1:T(1,128)}, u32[]{:S(2)}) copy-start(s32[16384,1]{0,1:T(1,128)} %param.9) | copy-start | bytes 196612
  3.7 36.2 %copy-start.1 = (s32[16384]{0:T(1024)S(1)}, s32[16384]{0:T(1024)}, u32[]{:S(2)}) copy-start(s32[16384]{0:T(1024)} %param.10) | copy-start | bytes 196612
  3.7 37.4 %collective-permute-start.2 = (bf16[128,8192]{1,0:T(8,128)(2,1)}, bf16[128,8192]{1,0:T(8,128)(2,1)S(1)}, u32[]{:S(2)}, u32[]{:S(2)}) collective-permute-start(bf16[128,8192]{1,0:T(8,128)(2,1)} %shard_map.98), channel_id=1, source_target_pairs={{0,16},{1,17},{2,18},{3,19},{4,20},{5,21},{6,22},{7,23},{8,24},{9,... | collective-permute-start | bytes 6291464 | tf_op jit(solution)/shard_map/ppermute | solution.py:50
  6.1 5.7 %collective-permute-start = (bf16[1,144,256]{2,1,0:T(8,128)(2,1)S(1)}, bf16[1,144,256]{2,1,0:T(8,128)(2,1)S(1)}, u32[]{:S(2)}, u32[]{:S(2)}) collective-permute-start(bf16[1,144,256]{2,1,0:T(8,128)(2,1)S(1)} %shard_map.94.a), channel_id=1, source_target_pairs={{0,1},{1,0},{2,3},{3,2},{4,5},{5,4},{6,7},{7,6},{8,9},{9,8},{10,11... | collective-permute-start | bytes 221192 | tf_op jit(solution)/shard_map/ppermute | solution.py:50
  11.8 4.4 %collective-permute-start.1 = (bf16[2,144,256]{2,1,0:T(8,128)(2,1)S(1)}, bf16[2,144,256]{2,1,0:T(8,128)(2,1)S(1)}, u32[]{:S(2)}, u32[]{:S(2)}) collective-permute-start(bf16[2,144,256]{2,1,0:T(8,128)(2,1)S(1)} %shard_map.95.a), channel_id=1, source_target_pairs={{0,3},{1,2},{2,1},{3,0},{4,7},{5,6},{6,5},{7,4},{8,11},{9,10},{10,... | collective-permute-start | bytes 442376 | tf_op jit(solution)/shard_map/ppermute | solution.py:50
  16.2 5.3 %collective-permute-start.5 = (bf16[4,128,128]{2,1,0:T(8,128)(2,1)S(1)}, bf16[4,128,128]{2,1,0:T(8,128)(2,1)S(1)}, u32[]{:S(2)}, u32[]{:S(2)}) collective-permute-start(bf16[4,128,128]{2,1,0:T(8,128)(2,1)S(1)} %get-tuple-element.25.a), channel_id=1, source_target_pairs={{0,4},{1,5},{2,6},{3,7},{4,0},{5,1},{6,2},{7,3},{8,12},{9,13},{10,... | collective-permute-start | bytes 393224 | tf_op jit(solution)/shard_map/ppermute | solution.py:50
  19.0 5.0 %collective-permute-start.3 = (bf16[4,128,128]{2,1,0:T(8,128)(2,1)S(1)}, bf16[4,128,128]{2,1,0:T(8,128)(2,1)S(1)}, u32[]{:S(2)}, u32[]{:S(2)}) collective-permute-start(bf16[4,128,128]{2,1,0:T(8,128)(2,1)S(1)} %get-tuple-element.24.a), channel_id=1, source_target_pairs={{0,32},{1,33},{2,34},{3,35},{4,36},{5,37},{6,38},{7,39},{8,40},{9,... | collective-permute-start | bytes 393224 | tf_op jit(solution)/shard_map/ppermute | solution.py:50
  21.5 5.3 %collective-permute-start.6 = (bf16[8,128,128]{2,1,0:T(8,128)(2,1)S(1)}, bf16[8,128,128]{2,1,0:T(8,128)(2,1)S(1)}, u32[]{:S(2)}, u32[]{:S(2)}) collective-permute-start(bf16[8,128,128]{2,1,0:T(8,128)(2,1)S(1)} %shard_map.101.a), channel_id=1, source_target_pairs={{0,12},{1,13},{2,14},{3,15},{4,8},{5,9},{6,10},{7,11},{8,4},{9,5},... | collective-permute-start | bytes 786440 | tf_op jit(solution)/shard_map/ppermute | solution.py:50
  24.1 5.6 %collective-permute-start.4 = (bf16[8,128,128]{2,1,0:T(8,128)(2,1)S(1)}, bf16[8,128,128]{2,1,0:T(8,128)(2,1)S(1)}, u32[]{:S(2)}, u32[]{:S(2)}) collective-permute-start(bf16[8,128,128]{2,1,0:T(8,128)(2,1)S(1)} %shard_map.99.a), channel_id=1, source_target_pairs={{0,96},{1,97},{2,98},{3,99},{4,100},{5,101},{6,102},{7,103},{8,104... | collective-permute-start | bytes 786440 | tf_op jit(solution)/shard_map/ppermute | solution.py:50
  26.9 12.0 %collective-permute-start.9 = (bf16[16,128,128]{2,1,0:T(8,128)(2,1)S(1)}, bf16[16,128,128]{2,1,0:T(8,128)(2,1)}, u32[]{:S(2)}, u32[]{:S(2)}) collective-permute-start(bf16[16,128,128]{2,1,0:T(8,128)(2,1)S(1)} %shard_map.102.b), channel_id=1, source_target_pairs={{0,32},{1,33},{2,34},{3,35},{4,36},{5,37},{6,38},{7,39},{8,40},{9,... | collective-permute-start | bytes 1572872 | tf_op jit(solution)/shard_map/ppermute | solution.py:50
  29.7 9.4 %collective-permute-start.7 = (bf16[16,128,128]{2,1,0:T(8,128)(2,1)S(1)}, bf16[16,128,128]{2,1,0:T(8,128)(2,1)}, u32[]{:S(2)}, u32[]{:S(2)}) collective-permute-start(bf16[16,128,128]{2,1,0:T(8,128)(2,1)S(1)} %shard_map.100.a), channel_id=1, source_target_pairs={{0,4},{1,5},{2,6},{3,7},{4,0},{5,1},{6,2},{7,3},{8,12},{9,13},{10,... | collective-permute-start | bytes 1572872 | tf_op jit(solution)/shard_map/ppermute | solution.py:50
  32.1 12.0 %collective-permute-start.11 = (bf16[16,128,128]{2,1,0:T(8,128)(2,1)S(1)}, bf16[16,128,128]{2,1,0:T(8,128)(2,1)}, u32[]{:S(2)}, u32[]{:S(2)}) collective-permute-start(bf16[16,128,128]{2,1,0:T(8,128)(2,1)S(1)} %shard_map.100.a), channel_id=1, source_target_pairs={{0,12},{1,13},{2,14},{3,15},{4,8},{5,9},{6,10},{7,11},{8,4},{9,5},... | collective-permute-start | bytes 1572872 | tf_op jit(solution)/shard_map/ppermute | solution.py:50
  32.1 13.2 %collective-permute-start.12 = (bf16[16,128,128]{2,1,0:T(8,128)(2,1)S(1)}, bf16[16,128,128]{2,1,0:T(8,128)(2,1)}, u32[]{:S(2)}, u32[]{:S(2)}) collective-permute-start(bf16[16,128,128]{2,1,0:T(8,128)(2,1)S(1)} %shard_map.102.b), channel_id=1, source_target_pairs={{0,96},{1,97},{2,98},{3,99},{4,100},{5,101},{6,102},{7,103},{8,104... | collective-permute-start | bytes 1572872 | tf_op jit(solution)/shard_map/ppermute | solution.py:50
  38.8 12.1 %collective-permute-start.10 = (bf16[16,128,128]{2,1,0:T(8,128)(2,1)}, bf16[16,128,128]{2,1,0:T(8,128)(2,1)}, u32[]{:S(2)}, u32[]{:S(2)}) collective-permute-start(bf16[16,128,128]{2,1,0:T(8,128)(2,1)} %collective-permute-done.9.b), channel_id=1, source_target_pairs={{0,96},{1,97},{2,98},{3,99},{4,100},{5,101},{6,102},{7,103},{8,104... | collective-permute-start | bytes 1572872 | tf_op jit(solution)/shard_map/ppermute | solution.py:50
  39.1 12.6 %collective-permute-start.8 = (bf16[16,128,128]{2,1,0:T(8,128)(2,1)}, bf16[16,128,128]{2,1,0:T(8,128)(2,1)}, u32[]{:S(2)}, u32[]{:S(2)}) collective-permute-start(bf16[16,128,128]{2,1,0:T(8,128)(2,1)} %collective-permute-done.7.a), channel_id=1, source_target_pairs={{0,12},{1,13},{2,14},{3,15},{4,8},{5,9},{6,10},{7,11},{8,4},{9,5},... | collective-permute-start | bytes 1572872 | tf_op jit(solution)/shard_map/ppermute | solution.py:50
  54.1 10.7 %collective-permute-start.13 = (f32[256,256]{1,0:T(8,128)S(1)}, f32[256,256]{1,0:T(8,128)S(1)}, u32[]{:S(2)}, u32[]{:S(2)}) collective-permute-start(f32[256,256]{1,0:T(8,128)S(1)} %get-tuple-element.29), channel_id=1, source_target_pairs={{0,16},{1,17},{2,18},{3,19},{4,20},{5,21},{6,22},{7,23},{8,24},{9,... | collective-permute-start | bytes 786440 | tf_op jit(solution)/shard_map/ppermute | solution.py:50
  65.6 18.9 %all-to-all-start = ((bf16[64,16,256]{2,1,0:T(8,128)(2,1)}), bf16[64,16,256]{2,1,0:T(8,128)(2,1)S(1)}, u32[]{:S(2)}, u32[]{:S(2)}) async-start(bf16[64,16,256]{2,1,0:T(8,128)(2,1)} %bitcast.14), calls=%async_computation | async-start | bytes 1048576 | tf_op jit(solution)/shard_map/all_to_all | solution.py:585
  84.8 6.6 %collective-permute-start.14 = (f32[128,256]{1,0:T(8,128)S(1)}, f32[128,256]{1,0:T(8,128)S(1)}, u32[]{:S(2)}, u32[]{:S(2)}) collective-permute-start(f32[128,256]{1,0:T(8,128)S(1)} %shard_map.107.top.current), channel_id=1, source_target_pairs={{0,4},{1,5},{2,6},{3,7},{4,0},{5,1},{6,2},{7,3},{8,12},{9,13},{10,... | collective-permute-start | bytes 393224 | tf_op jit(solution)/shard_map/ppermute | solution.py:50
